TPU v7x, 768 devices: a whole 4x8x12 slice. The times are simulated.
768 devices in a mesh: row: 8 (over x, core), col: 96 (over z, y).
Axes of the slice: x: 4, y: 8, z: 12, core: 2. Of those that a mesh axis runs over, the one named last changes fastest.
Arguments:
- features: float32 [3, 8, 512, 768], P(None, 'row'), may hold values from -6 to 6
- ridge: float32 [3, 8, 512], P(None, 'row'), may hold values from 0.5 to 4
Outputs:
- schur: float32 [3, 8, 512, 1, 96, 128], P(None, 'row', None, None, 'col')
- panel: float32 [3, 8, 512, 512], P(None, 'row')
All inputs are finite; a program needn't handle non-finite values.
Results may differ from a plain program's by a relative error of at most 0.00017.
Values sent between devices are 32-bit elements; how exact they have to be, the bound alone decides.
No kernel may reach another device: no remote copies, remote signals or barrier semaphores. Data moves between devices by JAX's collectives and lax.ppermute only.
A program may use at most 64 MiB of HBM per device.

v0:
```python
import jax
import jax.numpy as jnp
from jax import lax
from jax.experimental import pallas as pl
from jax.experimental.pallas import tpu as pltpu
from jax.sharding import PartitionSpec as P

F32 = jnp.float32
BF16 = jnp.bfloat16
NB = 128
TN = (((1,), (1,)), ((), ()))


def split(a):
    hi = a.astype(BF16)
    return hi, (a - hi.astype(F32)).astype(BF16)


def dot3(a, b):
    one = lambda x, y: lax.dot_general(x, y, TN, preferred_element_type=F32)
    return one(a[0], b[0]) + (one(a[0], b[1]) + one(a[1], b[0]))


def dotf(a, b):
    return lax.dot_general(
        a, b, TN, precision=lax.Precision.HIGHEST, preferred_element_type=F32
    )


def lanes(v, k):
    return jnp.broadcast_to(v[:, k : k + 1], (8, NB))


def micro(upper, inv, t, cols_ref):
    row, low, o = upper[t], inv[t], 8 * t
    for k in range(8):
        cols_ref[8 * k : 8 * k + 8, :] = lanes(row, o + k)
    s = {}
    for k in range(8):
        for i in range(k, 8):
            s[i, k] = jnp.broadcast_to(cols_ref[8 * k + i : 8 * k + i + 1, :], (8, NB))
    v = [jnp.broadcast_to(row[i : i + 1, :], (8, NB)) for i in range(8)]
    w = [jnp.broadcast_to(low[i : i + 1, :], (8, NB)) for i in range(8)]
    u = {r: [lanes(upper[r], o + k) for k in range(8)] for r in range(t + 1, 16)}
    scale = []
    for k in range(8):
        rs = lax.rsqrt(s[k, k])
        scale.append(rs)
        v[k] = v[k] * rs
        w[k] = w[k] * rs
        for i in range(k + 1, 8):
            s[i, k] = s[i, k] * rs
        for j in range(k + 1, 8):
            for i in range(j, 8):
                s[i, j] = s[i, j] - s[i, k] * s[j, k]
        for i in range(k + 1, 8):
            v[i] = v[i] - s[i, k] * v[k]
            w[i] = w[i] - s[i, k] * w[k]
    upper, inv = list(upper), list(inv)
    if t < 15:
        r = t + 1
        for k in range(8):
            c = u[r][k]
            for m in range(k):
                c = c - u[r][m] * s[k, m]
            c = c * scale[k]
            u[r][k] = c
            upper[r] = upper[r] - c * v[k]
            inv[r] = inv[r] - c * w[k]
    if t < 14:
        vb, wb = list(v), list(w)
        for k in range(7, -1, -1):
            for m in range(k + 1, 8):
                vb[k] = vb[k] - s[m, k] * vb[m]
                wb[k] = wb[k] - s[m, k] * wb[m]
            vb[k] = vb[k] * scale[k]
            wb[k] = wb[k] * scale[k]
        for r in range(t + 2, 16):
            for k in range(8):
                upper[r] = upper[r] - u[r][k] * vb[k]
                inv[r] = inv[r] - u[r][k] * wb[k]
    sub = lax.broadcasted_iota(jnp.int32, (8, NB), 0)
    a, b = v[0], w[0]
    for k in range(1, 8):
        a = jnp.where(sub == k, v[k], a)
        b = jnp.where(sub == k, w[k], b)
    upper[t], inv[t] = a, b
    return upper, inv


def factor(block, cols_ref, work=()):
    upper = [block[8 * i : 8 * i + 8, :] for i in range(16)]
    sub = lax.broadcasted_iota(jnp.int32, (8, NB), 0)
    lane = lax.broadcasted_iota(jnp.int32, (8, NB), 1)
    inv = [jnp.where(lane == sub + 8 * i, F32(1.0), F32(0.0)) for i in range(16)]
    for t in range(16):
        for job in work[len(work) * t // 16 : len(work) * (t + 1) // 16]:
            job()
        upper, inv = micro(upper, inv, t, cols_ref.at[64 * (t % 2) : 64 * (t % 2) + 64])
    return upper, inv


def tile_of(inner, width):
    return jnp.square(inner / width + 1.0)


def match(shape, delta):
    rows = lax.broadcasted_iota(jnp.int32, shape, 0)
    cols = lax.broadcasted_iota(jnp.int32, shape, 1)
    return rows - cols == delta


def kernel_tile(left, right, delta, ridge, feat):
    block = tile_of(dot3(left, right), feat)
    return block + jnp.where(match(block.shape, delta), ridge, F32(0.0))


STEP = 192
FAR = 1 << 20


def first_kernel(
    where_ref, rows_hbm, a_ref, b_ref,
    panel_hbm, p_hi, p_lo, pan_hi, pan_lo, line_ref, inv_hi, inv_lo, low_hi, low_lo,
    rows, kp, out, cols_ref, in_sem, out_sem,
):
    count, feat = rows.shape
    half = kp.shape[1]
    load = pltpu.make_async_copy(rows_hbm, rows, in_sem)
    load.start()
    row_idx = where_ref[0]
    pan_hi[...], pan_lo[...] = split(a_ref[:half, :] + b_ref[:half, :])
    line = a_ref[half : half + 1, :half] + b_ref[half : half + 1, :half]
    line_ref[...] = jnp.broadcast_to(line, (8, half))
    pan = (pan_hi[...], pan_lo[...])
    k11 = kernel_tile(pan, (pan_hi[:NB, :], pan_lo[:NB, :]), 0, line[:, :NB], feat)
    k22 = kernel_tile(
        (pan_hi[NB:, :], pan_lo[NB:, :]), (pan_hi[NB:, :], pan_lo[NB:, :]), 0, line[:, NB:], feat
    )
    load.wait()

    def tiles(i):
        n = i * STEP
        x = split(rows[n : n + STEP, :])
        g = tile_of(dot3(x, (pan_hi[...], pan_lo[...])), feat)
        if n < 512:
            g = g + jnp.where(match(g.shape, jnp.where(row_idx == 0, -n, FAR)), line, F32(0.0))
        kp[n : n + STEP, :] = g

    _, inv = factor(k11[:NB], cols_ref, [lambda i=i: tiles(i) for i in range(count // STEP)])
    inv0 = jnp.concatenate(inv, axis=0)
    inv_hi[0], inv_lo[0] = split(inv0)
    l10 = dotf(k11[NB:], inv0)
    low_hi[...], low_lo[...] = split(l10)
    s11 = k22 - dotf(l10, l10)

    def solve(i):
        n = i * STEP
        x = dot3(split(kp[n : n + STEP, :NB]), (inv_hi[0], inv_lo[0]))
        out[n : n + STEP, :NB] = x
        hi, lo = split(x)
        p_hi[n : n + STEP, :NB], p_lo[n : n + STEP, :NB] = hi, lo
        kp[n : n + STEP, NB:] = kp[n : n + STEP, NB:] - dot3((hi, lo), (low_hi[...], low_lo[...]))

    _, inv = factor(s11, cols_ref, [lambda i=i: solve(i) for i in range(count // STEP)])
    inv_hi[1], inv_lo[1] = split(jnp.concatenate(inv, axis=0))
    x = dot3(split(kp[:, NB:]), (inv_hi[1], inv_lo[1]))
    out[:, NB:] = x
    p_hi[:, NB:], p_lo[:, NB:] = split(x)
    store = pltpu.make_async_copy(out, panel_hbm.at[:, pl.ds(0, half)], out_sem)
    store.start()
    store.wait()


def second_kernel(
    where_ref, rows_hbm, a_ref, b_ref, ca_ref, cb_ref, ridge_ref, old_panel,
    p_hi, p_lo, pan_hi, pan_lo, line_ref, inv_hi, inv_lo, low_hi, low_lo,
    schur_ref, panel_hbm,
    rows, kp, out, q_hi, q_lo, l2_hi, l2_lo, l32_hi, l32_lo, nv_hi, nv_lo, col_hi, col_lo, kc, pc_hi, pc_lo,
    cols_ref, in_sem, out_sem,
):
    count, feat = rows.shape
    half = kp.shape[1]
    load = pltpu.make_async_copy(rows_hbm, rows, in_sem)
    load.start()
    row_idx, col_idx = where_ref[0], where_ref[1]
    q_hi[...], q_lo[...] = split(a_ref[:half, :] + b_ref[:half, :])
    line = a_ref[half : half + 1, :half] + b_ref[half : half + 1, :half]
    col_hi[...], col_lo[...] = split(ca_ref[...] + cb_ref[...])
    new = (q_hi[...], q_lo[...])

    def lead(k, dst_hi, dst_lo):
        n0 = dot3(split(k[:, :NB]), (inv_hi[0], inv_lo[0]))
        s0 = split(n0)
        n1 = dot3(split(k[:, NB:] - dot3(s0, (low_hi[...], low_lo[...]))), (inv_hi[1], inv_lo[1]))
        s1 = split(n1)
        dst_hi[:, :NB], dst_lo[:, :NB] = s0
        dst_hi[:, NB:half], dst_lo[:, NB:half] = s1

    lead(tile_of(dot3(new, (pan_hi[...], pan_lo[...])), feat), l2_hi, l2_lo)
    k2 = kernel_tile(new, new, 0, line, feat) - dot3((l2_hi[...], l2_lo[...]), (l2_hi[...], l2_lo[...]))
    load.wait()

    def tiles(i):
        n = i * STEP
        x = split(rows[n : n + STEP, :])
        g = tile_of(dot3(x, (q_hi[...], q_lo[...])), feat)
        if half - n > -STEP and n < 512:
            g = g + jnp.where(match(g.shape, jnp.where(row_idx == 0, half - n, FAR)), line, F32(0.0))
        kp[n : n + STEP, :] = g - dot3(
            (p_hi[n : n + STEP, :], p_lo[n : n + STEP, :]), (l2_hi[...], l2_lo[...])
        )

    _, inv = factor(k2[:NB, :NB], cols_ref, [lambda i=i: tiles(i) for i in range(count // STEP)])
    inv2 = jnp.concatenate(inv, axis=0)
    nv_hi[0], nv_lo[0] = split(inv2)
    l32 = dotf(k2[NB:, :NB], inv2)
    l32_hi[...], l32_lo[...] = split(l32)
    s33 = k2[NB:, NB:] - dotf(l32, l32)
    first = col_idx * NB
    owner, n_tile = (col_idx // 4) % 8, col_idx // 32
    inner = (col_idx % 4) * NB
    diag = ridge_ref[n_tile, :, pl.ds(pl.multiple_of(inner, NB), NB)]
    corner = jnp.where(row_idx == owner, n_tile * 512 + inner, FAR)

    def columns():
        col = (col_hi[...], col_lo[...])
        lead(
            kernel_tile(col, (pan_hi[...], pan_lo[...]), -first, line_ref[:1, :], feat),
            pc_hi, pc_lo,
        )
        kc[...] = kernel_tile(col, new, half - first, line, feat) - dot3(
            (pc_hi[:, :half], pc_lo[:, :half]), (l2_hi[...], l2_lo[...])
        )
        x = split(dot3(split(kc[:, :NB]), (nv_hi[0], nv_lo[0])))
        pc_hi[:, half : half + NB], pc_lo[:, half : half + NB] = x
        kc[:, NB:] = kc[:, NB:] - dot3(x, (l32_hi[...], l32_lo[...]))

    def solve(i):
        n = i * STEP
        x = dot3(split(kp[n : n + STEP, :NB]), (nv_hi[0], nv_lo[0]))
        out[n : n + STEP, :NB] = x
        s = split(x)
        kp[n : n + STEP, NB:] = kp[n : n + STEP, NB:] - dot3(s, (l32_hi[...], l32_lo[...]))
        g = tile_of(dot3(split(rows[n : n + STEP, :]), (col_hi[...], col_lo[...])), feat)
        g = g + jnp.where(match(g.shape, corner - n), diag, F32(0.0))
        g = g - dot3(
            (p_hi[n : n + STEP, :], p_lo[n : n + STEP, :]), (pc_hi[:, :half], pc_lo[:, :half])
        )
        schur_ref[n : n + STEP, :] = g - dot3(
            s, (pc_hi[:, half : half + NB], pc_lo[:, half : half + NB])
        )

    _, inv = factor(
        s33, cols_ref, [columns] + [lambda i=i: solve(i) for i in range(count // STEP)]
    )
    nv_hi[1], nv_lo[1] = split(jnp.concatenate(inv, axis=0))
    pc = split(dot3(split(kc[:, NB:]), (nv_hi[1], nv_lo[1])))
    x = dot3(split(kp[:, NB:]), (nv_hi[1], nv_lo[1]))
    out[:, NB:] = x
    store = pltpu.make_async_copy(out, panel_hbm.at[:, pl.ds(half, half)], out_sem)
    store.start()
    schur_ref[...] = schur_ref[...] - dot3(split(x), pc)
    store.wait()


VM = pl.BlockSpec(memory_space=pltpu.VMEM)
SM = pl.BlockSpec(memory_space=pltpu.SMEM)
HB = pl.BlockSpec(memory_space=pltpu.HBM)


def shaped(*shape, kind=F32):
    return jax.ShapeDtypeStruct(shape, kind)


def first_step(where, rows, pair):
    count, feat = rows.shape
    half = 256
    return pl.pallas_call(
        first_kernel,
        out_shape=(
            shaped(count, 2 * half),
            shaped(count, half, kind=BF16),
            shaped(count, half, kind=BF16),
            shaped(half, feat, kind=BF16),
            shaped(half, feat, kind=BF16),
            shaped(8, half),
            shaped(2, NB, NB, kind=BF16),
            shaped(2, NB, NB, kind=BF16),
            shaped(NB, NB, kind=BF16),
            shaped(NB, NB, kind=BF16),
        ),
        in_specs=[SM, HB, VM, VM],
        out_specs=(HB,) + (VM,) * 9,
        scratch_shapes=[
            pltpu.VMEM((count, feat), F32),
            pltpu.VMEM((count, half), F32),
            pltpu.VMEM((count, half), F32),
            pltpu.VMEM((NB, NB), F32),
            pltpu.SemaphoreType.DMA,
            pltpu.SemaphoreType.DMA,
        ],
        compiler_params=pltpu.CompilerParams(vmem_limit_bytes=20 << 20),
        cost_estimate=pl.CostEstimate(flops=5 * 10**9, bytes_accessed=40 * 10**6, transcendentals=0),
        name="first_step",
    )(where, rows, *pair)


def second_step(where, rows, pair, cols, ridge, kept):
    count, feat = rows.shape
    half = 256
    return pl.pallas_call(
        second_kernel,
        out_shape=(shaped(count, NB), shaped(count, 2 * half)),
        in_specs=[SM, HB] + [VM] * 5 + [HB] + [VM] * 9,
        out_specs=(VM, HB),
        input_output_aliases={7: 1},
        scratch_shapes=[
            pltpu.VMEM((count, feat), F32),
            pltpu.VMEM((count, half), F32),
            pltpu.VMEM((count, half), F32),
            pltpu.VMEM((half, feat), BF16),
            pltpu.VMEM((half, feat), BF16),
            pltpu.VMEM((half, half), BF16),
            pltpu.VMEM((half, half), BF16),
            pltpu.VMEM((NB, NB), BF16),
            pltpu.VMEM((NB, NB), BF16),
            pltpu.VMEM((2, NB, NB), BF16),
            pltpu.VMEM((2, NB, NB), BF16),
            pltpu.VMEM((NB, feat), BF16),
            pltpu.VMEM((NB, feat), BF16),
            pltpu.VMEM((NB, half), F32),
            pltpu.VMEM((NB, half + NB), BF16),
            pltpu.VMEM((NB, half + NB), BF16),
            pltpu.VMEM((NB, NB), F32),
            pltpu.SemaphoreType.DMA,
            pltpu.SemaphoreType.DMA,
        ],
        compiler_params=pltpu.CompilerParams(vmem_limit_bytes=20 << 20),
        cost_estimate=pl.CostEstimate(flops=5 * 10**9, bytes_accessed=40 * 10**6, transcendentals=0),
        name="second_step",
    )(where, rows, *pair, *cols, ridge, *kept)


def prepare_kernel(where_ref, feats_ref, ridge_ref, own0, own1, piece, sems):
    half = own0.shape[0] - 8
    loads = [
        pltpu.make_async_copy(feats_ref.at[0, pl.ds(0, half)], own0.at[pl.ds(0, half)], sems.at[0]),
        pltpu.make_async_copy(feats_ref.at[0, pl.ds(half, half)], own1.at[pl.ds(0, half)], sems.at[1]),
        pltpu.make_async_copy(
            feats_ref.at[where_ref[1] // 32, pl.ds(pl.multiple_of(where_ref[1] % 4 * NB, NB), NB)],
            piece,
            sems.at[2],
        ),
    ]
    for load in loads:
        load.start()
    for h, own in enumerate((own0, own1)):
        own[half:, :half] = jnp.broadcast_to(ridge_ref[0, :, h * half : (h + 1) * half], (8, half))
        own[half:, half:] = jnp.zeros((8, own.shape[1] - half), F32)
    for load in loads:
        load.wait()


def prepare(where, feats, ridge):
    half, feat = 256, feats.shape[2]
    return pl.pallas_call(
        prepare_kernel,
        out_shape=(shaped(half + 8, feat), shaped(half + 8, feat), shaped(NB, feat)),
        in_specs=[SM, HB, VM],
        out_specs=(VM, VM, VM),
        scratch_shapes=[pltpu.SemaphoreType.DMA((3,))],
        name="prepare",
    )(where, feats, ridge)


def moved(block, hop):
    links = []
    for device in range(768):
        x, c, z, y = device // 192, device // 96 % 2, device % 96 // 8, device % 8
        to = hop(x, c, y, z)
        if to is not None:
            links.append((device, (to[0] % 4 * 2 + to[1]) * 96 + z * 8 + y))
    return lax.ppermute(block, ("row", "col"), links)


def along(start, stop):
    return lambda x, c, y, z: (stop, 0) if (x, c) == (start, 0) else None


def fanned(step):
    return lambda x, c, y, z: (x + step, c) if (x, c) == (z % 4, y // 4) else None


def per_device(features, ridge):
    tiles, _, width, feat = features.shape
    row_idx = lax.axis_index("row")
    col_idx = lax.axis_index("col")
    where = jnp.stack([row_idx, col_idx]).astype(jnp.int32)
    feats = features.reshape(tiles, width, feat)
    own0, own1, piece = prepare(where, feats, ridge)
    g0 = moved(own0, along(0, 3))
    f0 = moved(own0, along(0, 1))
    d0 = moved(own0, along(0, 2))
    g1 = moved(own1, along(0, 3))
    f1 = moved(own1, along(0, 1))
    c1 = moved(piece, fanned(1))
    c2 = moved(piece, fanned(3))
    c3 = moved(piece, fanned(2))
    a0 = jnp.where(row_idx == 0, own0, F32(0.0)) + f0 + g0 + d0
    b0 = moved(a0, lambda x, c, y, z: (x, 1) if c == 0 else None)
    h1 = moved(g1, along(3, 2))
    rows = pltpu.with_memory_space_constraint(feats.reshape(tiles * width, feat), pltpu.HBM)
    kept = first_step(where, rows, (a0, b0))
    a1 = jnp.where(row_idx == 0, own1, F32(0.0)) + f1 + g1 + h1
    b1 = moved(a1, lambda x, c, y, z: (x, 1) if c == 0 else None)
    holder = row_idx == col_idx // 4 % 8
    ca = jnp.where(holder, piece, F32(0.0)) + c1 + c2 + c3
    cb = moved(ca, lambda x, c, y, z: (x, 1 - c) if c == y // 4 else None)
    schur, panel = second_step(where, rows, (a1, b1), (ca, cb), ridge, kept)
    return (
        schur.reshape(tiles, 1, width, 1, 1, NB),
        panel.reshape(tiles, 1, width, width),
    )


def solution(mesh):
    in_specs = (P(None, "row", None, None), P(None, "row", None))
    out_specs = (P(None, "row", None, None, "col", None), P(None, "row", None, None))
    return jax.shard_map(
        per_device, mesh=mesh, in_specs=in_specs, out_specs=out_specs, check_vma=False
    )
```

profile of v0, /device:TPU:2, one launch (start us, length us, event | category | flops | bytes accessed | tf_op | source)
XLA Modules:
  0.0 90.0 jit_solution(16534920904677841521)
XLA Ops:
  0.6 0.6 pad_add_fusion.where_ref
  1.3 3.5 %prepare.1 = (f32[264,768]{1,0:T(8,128)}, f32[264,768]{1,0:T(8,128)}, f32[128,768]{1,0:T(8,128)}) custom-call(s32[2]{0:T(128)} %pad_add_fusion.where_ref, f32[3,512,768]{2,1,0:T(8,128)} %bitcast.10, f32[3,1,512]{2,1,0:T(1,128)} %ridge_ref.3), custom_call_target="tpu_custom_call" | custom-call | tf_op jit(solution)/shard_map/prepare/pallas_call | solution.py:367
  4.7 0.8 collective-permute-start.1
  5.6 0.7 collective-permute-start.10
  6.3 0.7 collective-permute-start.9
  7.0 1.3 %collective-permute-start.8 = (f32[264,768]{1,0:T(8,128)}, f32[264,768]{1,0:T(8,128)}, u32[]{:S(2)}, u32[]{:S(2)}) collective-permute-start(f32[264,768]{1,0:T(8,128)} %get-tuple-element.19), channel_id=1, source_target_pairs={{0,192},{1,193},{2,194},{3,195},{4,196},{5,197},{6,198},{7,199},{8... | collective-permute-start | bytes 2433032 | tf_op jit(solution)/shard_map/ppermute | solution.py:384
  8.3 1.3 %collective-permute-start = (f32[264,768]{1,0:T(8,128)}, f32[264,768]{1,0:T(8,128)}, u32[]{:S(2)}, u32[]{:S(2)}) collective-permute-start(f32[264,768]{1,0:T(8,128)} %get-tuple-element.17), channel_id=1, source_target_pairs={{0,192},{1,193},{2,194},{3,195},{4,196},{5,197},{6,198},{7,199},{8... | collective-permute-start | bytes 2433032 | tf_op jit(solution)/shard_map/ppermute | solution.py:384
  9.6 0.0 collective-permute-done.1
  9.7 1.6 %collective-permute-start.2 = (f32[264,768]{1,0:T(8,128)S(1)}, f32[264,768]{1,0:T(8,128)}, u32[]{:S(2)}, u32[]{:S(2)}) collective-permute-start(f32[264,768]{1,0:T(8,128)S(1)} %collective-permute-done.1), channel_id=1, source_target_pairs={{576,384},{577,385},{578,386},{579,387},{580,388},{581,389},{582,3... | collective-permute-start | bytes 2433032 | tf_op jit(solution)/shard_map/ppermute | solution.py:384
  11.3 0.0 collective-permute-done.10
  11.3 0.0 collective-permute-done.9
  11.3 0.9 %copy-done.4 = f32[264,768]{1,0:T(8,128)} copy-done((f32[264,768]{1,0:T(8,128)}, f32[264,768]{1,0:T(8,128)S(1)}, u32[]{:S(2)}) %copy-start.4) | copy-done | bytes 811032
  12.2 24.1 %collective-permute-done.8 = f32[264,768]{1,0:T(8,128)} collective-permute-done((f32[264,768]{1,0:T(8,128)}, f32[264,768]{1,0:T(8,128)}, u32[]{:S(2)}, u32[]{:S(2)}) %collective-permute-start.8) | collective-permute-done | bytes 811040 | tf_op jit(solution)/shard_map/ppermute | solution.py:384
  36.3 1.6 %add_add_fusion.a_ref = f32[264,768]{1,0:T(8,128)S(1)} fusion(f32[264,768]{1,0:T(8,128)S(1)} %collective-permute-done.10, f32[264,768]{1,0:T(8,128)} %copy-done.4, f32[264,768]{1,0:T(8,128)} %collective-permute-done.8, f32[264,768]{1,0:T(8,128)} %get-tuple-element.19, pred[]{:T(512)S(6)} %eq.9), kind=kLoop, calls=%fused_computation | loop fusion | flops 811008 | bytes 4055041 | tf_op jit(solution)/shard_map/add | solution.py:410
  37.9 1.3 %collective-permute-start.11 = (f32[264,768]{1,0:T(8,128)S(1)}, f32[264,768]{1,0:T(8,128)S(1)}, u32[]{:S(2)}, u32[]{:S(2)}) collective-permute-start(f32[264,768]{1,0:T(8,128)S(1)} %add_add_fusion.a_ref), channel_id=1, source_target_pairs={{0,96},{1,97},{2,98},{3,99},{4,100},{5,101},{6,102},{7,103},{8,104... | collective-permute-start | bytes 2433032 | tf_op jit(solution)/shard_map/ppermute | solution.py:384
  39.3 1.4 %collective-permute-start.6 = (f32[128,768]{1,0:T(8,128)}, f32[128,768]{1,0:T(8,128)}, u32[]{:S(2)}, u32[]{:S(2)}) collective-permute-start(f32[128,768]{1,0:T(8,128)} %get-tuple-element.18), channel_id=1, source_target_pairs={{0,384},{1,385},{2,386},{3,387},{32,416},{33,417},{34,418},{35,419... | collective-permute-start | bytes 1179656 | tf_op jit(solution)/shard_map/ppermute | solution.py:384
  40.7 1.4 %collective-permute-start.5 = (f32[128,768]{1,0:T(8,128)}, f32[128,768]{1,0:T(8,128)}, u32[]{:S(2)}, u32[]{:S(2)}) collective-permute-start(f32[128,768]{1,0:T(8,128)} %get-tuple-element.18), channel_id=1, source_target_pairs={{0,576},{1,577},{2,578},{3,579},{32,608},{33,609},{34,610},{35,611... | collective-permute-start | bytes 1179656 | tf_op jit(solution)/shard_map/ppermute | solution.py:384
  42.1 2.9 %collective-permute-done = f32[264,768]{1,0:T(8,128)} collective-permute-done((f32[264,768]{1,0:T(8,128)}, f32[264,768]{1,0:T(8,128)}, u32[]{:S(2)}, u32[]{:S(2)}) %collective-permute-start) | collective-permute-done | bytes 811040 | tf_op jit(solution)/shard_map/ppermute | solution.py:384
  44.9 1.3 %collective-permute-start.4 = (f32[128,768]{1,0:T(8,128)}, f32[128,768]{1,0:T(8,128)}, u32[]{:S(2)}, u32[]{:S(2)}) collective-permute-start(f32[128,768]{1,0:T(8,128)} %get-tuple-element.18), channel_id=1, source_target_pairs={{0,192},{1,193},{2,194},{3,195},{32,224},{33,225},{34,226},{35,227... | collective-permute-start | bytes 1179656 | tf_op jit(solution)/shard_map/ppermute | solution.py:384
  46.2 0.0 collective-permute-done.2
  46.3 1.9 %add_add_fusion.1.a_ref = f32[264,768]{1,0:T(8,128)S(1)} fusion(f32[264,768]{1,0:T(8,128)} %collective-permute-done.2, f32[264,768]{1,0:T(8,128)} %copy-done.3, f32[264,768]{1,0:T(8,128)} %collective-permute-done, f32[264,768]{1,0:T(8,128)S(1)} %copy-done.2, pred[]{:T(512)S(6)} %eq.9), kind=kLoop, calls=%fused_computation.1 | loop fusion | flops 811008 | bytes 4055041 | tf_op jit(solution)/shard_map/add | solution.py:415
  48.1 1.3 %collective-permute-start.3 = (f32[264,768]{1,0:T(8,128)S(1)}, f32[264,768]{1,0:T(8,128)S(1)}, u32[]{:S(2)}, u32[]{:S(2)}) collective-permute-start(f32[264,768]{1,0:T(8,128)S(1)} %add_add_fusion.1.a_ref), channel_id=1, source_target_pairs={{0,96},{1,97},{2,98},{3,99},{4,100},{5,101},{6,102},{7,103},{8,104... | collective-permute-start | bytes 2433032 | tf_op jit(solution)/shard_map/ppermute | solution.py:384
  49.5 0.0 collective-permute-done.6
  49.5 0.0 collective-permute-done.5
  49.6 5.4 %collective-permute-done.4 = f32[128,768]{1,0:T(8,128)} collective-permute-done((f32[128,768]{1,0:T(8,128)}, f32[128,768]{1,0:T(8,128)}, u32[]{:S(2)}, u32[]{:S(2)}) %collective-permute-start.4) | collective-permute-done | bytes 393248 | tf_op jit(solution)/shard_map/ppermute | solution.py:384
  54.9 1.3 %add_add_fusion.2.ca_ref = f32[128,768]{1,0:T(8,128)S(1)} fusion(f32[128,768]{1,0:T(8,128)} %collective-permute-done.6, f32[128,768]{1,0:T(8,128)} %collective-permute-done.5, f32[128,768]{1,0:T(8,128)} %collective-permute-done.4, f32[128,768]{1,0:T(8,128)} %get-tuple-element.18, pred[]{:T(512)S(6)} %eq.10), kind=kLoop, calls=%fused_computation.2 | loop fusion | flops 393216 | bytes 1966081 | tf_op jit(solution)/shard_map/add | solution.py:418
  56.2 1.3 %collective-permute-start.7 = (f32[128,768]{1,0:T(8,128)S(1)}, f32[128,768]{1,0:T(8,128)S(1)}, u32[]{:S(2)}, u32[]{:S(2)}) collective-permute-start(f32[128,768]{1,0:T(8,128)S(1)} %add_add_fusion.2.ca_ref), channel_id=1, source_target_pairs={{0,96},{1,97},{2,98},{3,99},{8,104},{9,105},{10,106},{11,107},{16,... | collective-permute-start | bytes 1179656 | tf_op jit(solution)/shard_map/ppermute | solution.py:384
  57.6 0.0 collective-permute-done.11.b_ref
  57.6 0.0 copy-start
  57.6 13.0 %first_step.1 = (f32[1536,512]{1,0:T(8,128)}, bf16[1536,256]{1,0:T(8,128)(2,1)S(1)}, bf16[1536,256]{1,0:T(8,128)(2,1)S(1)}, bf16[256,768]{1,0:T(8,128)(2,1)S(1)}...) custom-call(s32[2]{0:T(128)S(1)} %copy-done.1, ...), custom_call_target="tpu_custom_call" | custom-call | flops 5000000000 | bytes 40000000 | tf_op jit(solution)/shard_map/first_step/pallas_call | solution.py:279
  70.6 0.0 collective-permute-done.7.cb_ref
  70.6 19.2 %second_step.1 = (f32[1536,128]{1,0:T(8,128)}, f32[1536,512]{1,0:T(8,128)}) custom-call(s32[2]{0:T(128)S(1)} %copy-done.1, f32[1536,768]{1,0:T(8,128)} %bitcast.12, f32[264,768]{1,0:T(8,128)S(1)} %add_add_fusion.1.a_ref, f32[264,768]{1,0:T(8,128)S(1)} %collective-permute-done.3.b_ref, ...), custom_call_target="tpu_custom_call", output_to_operand_aliasing={{1}: (7, {})} | custom-call | flops 5000000000 | bytes 40000000 | tf_op jit(solution)/shard_map/second_step/pallas_call | solution.py:312
  (9 shorter events, 0.0 us)
Async XLA Ops:
  4.7 41.5 %copy-start.2 = (f32[264,768]{1,0:T(8,128)S(1)}, f32[264,768]{1,0:T(8,128)}, u32[]{:S(2)}) copy-start(f32[264,768]{1,0:T(8,128)} %get-tuple-element.17) | copy-start | bytes 2433028
  4.7 4.9 %collective-permute-start.1 = (f32[264,768]{1,0:T(8,128)}, f32[264,768]{1,0:T(8,128)S(1)}, u32[]{:S(2)}, u32[]{:S(2)}) collective-permute-start(f32[264,768]{1,0:T(8,128)} %get-tuple-element.17), channel_id=1, source_target_pairs={{0,576},{1,577},{2,578},{3,579},{4,580},{5,581},{6,582},{7,583},{8... | collective-permute-start | bytes 2433032 | tf_op jit(solution)/shard_map/ppermute | solution.py:384
  5.6 5.7 %collective-permute-start.10 = (f32[264,768]{1,0:T(8,128)}, f32[264,768]{1,0:T(8,128)S(1)}, u32[]{:S(2)}, u32[]{:S(2)}) collective-permute-start(f32[264,768]{1,0:T(8,128)} %get-tuple-element.19), channel_id=1, source_target_pairs={{0,384},{1,385},{2,386},{3,387},{4,388},{5,389},{6,390},{7,391},{8... | collective-permute-start | bytes 2433032 | tf_op jit(solution)/shard_map/ppermute | solution.py:384
  6.3 4.9 %collective-permute-start.9 = (f32[264,768]{1,0:T(8,128)}, f32[264,768]{1,0:T(8,128)S(1)}, u32[]{:S(2)}, u32[]{:S(2)}) collective-permute-start(f32[264,768]{1,0:T(8,128)} %get-tuple-element.19), channel_id=1, source_target_pairs={{0,576},{1,577},{2,578},{3,579},{4,580},{5,581},{6,582},{7,583},{8... | collective-permute-start | bytes 2433032 | tf_op jit(solution)/shard_map/ppermute | solution.py:384
  7.0 29.2 %collective-permute-start.8 = (f32[264,768]{1,0:T(8,128)}, f32[264,768]{1,0:T(8,128)}, u32[]{:S(2)}, u32[]{:S(2)}) collective-permute-start(f32[264,768]{1,0:T(8,128)} %get-tuple-element.19), channel_id=1, source_target_pairs={{0,192},{1,193},{2,194},{3,195},{4,196},{5,197},{6,198},{7,199},{8... | collective-permute-start | bytes 2433032 | tf_op jit(solution)/shard_map/ppermute | solution.py:384
  8.3 36.6 %collective-permute-start = (f32[264,768]{1,0:T(8,128)}, f32[264,768]{1,0:T(8,128)}, u32[]{:S(2)}, u32[]{:S(2)}) collective-permute-start(f32[264,768]{1,0:T(8,128)} %get-tuple-element.17), channel_id=1, source_target_pairs={{0,192},{1,193},{2,194},{3,195},{4,196},{5,197},{6,198},{7,199},{8... | collective-permute-start | bytes 2433032 | tf_op jit(solution)/shard_map/ppermute | solution.py:384
  9.6 36.6 %copy-start.3 = (f32[264,768]{1,0:T(8,128)}, f32[264,768]{1,0:T(8,128)S(1)}, u32[]{:S(2)}) copy-start(f32[264,768]{1,0:T(8,128)S(1)} %collective-permute-done.1) | copy-start | bytes 2433028
  9.7 36.6 %collective-permute-start.2 = (f32[264,768]{1,0:T(8,128)S(1)}, f32[264,768]{1,0:T(8,128)}, u32[]{:S(2)}, u32[]{:S(2)}) collective-permute-start(f32[264,768]{1,0:T(8,128)S(1)} %collective-permute-done.1), channel_id=1, source_target_pairs={{576,384},{577,385},{578,386},{579,387},{580,388},{581,389},{582,3... | collective-permute-start | bytes 2433032 | tf_op jit(solution)/shard_map/ppermute | solution.py:384
  11.3 0.9 %copy-start.4 = (f32[264,768]{1,0:T(8,128)}, f32[264,768]{1,0:T(8,128)S(1)}, u32[]{:S(2)}) copy-start(f32[264,768]{1,0:T(8,128)S(1)} %collective-permute-done.9) | copy-start | bytes 2433028
  37.9 19.7 %copy-start.1 = (s32[2]{0:T(128)S(1)}, s32[2]{0:T(128)}, u32[]{:S(2)}) copy-start(s32[2]{0:T(128)} %pad_add_fusion.where_ref) | copy-start | bytes 28
  37.9 19.7 %collective-permute-start.11 = (f32[264,768]{1,0:T(8,128)S(1)}, f32[264,768]{1,0:T(8,128)S(1)}, u32[]{:S(2)}, u32[]{:S(2)}) collective-permute-start(f32[264,768]{1,0:T(8,128)S(1)} %add_add_fusion.a_ref), channel_id=1, source_target_pairs={{0,96},{1,97},{2,98},{3,99},{4,100},{5,101},{6,102},{7,103},{8,104... | collective-permute-start | bytes 2433032 | tf_op jit(solution)/shard_map/ppermute | solution.py:384
  39.3 10.3 %collective-permute-start.6 = (f32[128,768]{1,0:T(8,128)}, f32[128,768]{1,0:T(8,128)}, u32[]{:S(2)}, u32[]{:S(2)}) collective-permute-start(f32[128,768]{1,0:T(8,128)} %get-tuple-element.18), channel_id=1, source_target_pairs={{0,384},{1,385},{2,386},{3,387},{32,416},{33,417},{34,418},{35,419... | collective-permute-start | bytes 1179656 | tf_op jit(solution)/shard_map/ppermute | solution.py:384
  40.7 8.9 %collective-permute-start.5 = (f32[128,768]{1,0:T(8,128)}, f32[128,768]{1,0:T(8,128)}, u32[]{:S(2)}, u32[]{:S(2)}) collective-permute-start(f32[128,768]{1,0:T(8,128)} %get-tuple-element.18), channel_id=1, source_target_pairs={{0,576},{1,577},{2,578},{3,579},{32,608},{33,609},{34,610},{35,611... | collective-permute-start | bytes 1179656 | tf_op jit(solution)/shard_map/ppermute | solution.py:384
  44.9 10.0 %collective-permute-start.4 = (f32[128,768]{1,0:T(8,128)}, f32[128,768]{1,0:T(8,128)}, u32[]{:S(2)}, u32[]{:S(2)}) collective-permute-start(f32[128,768]{1,0:T(8,128)} %get-tuple-element.18), channel_id=1, source_target_pairs={{0,192},{1,193},{2,194},{3,195},{32,224},{33,225},{34,226},{35,227... | collective-permute-start | bytes 1179656 | tf_op jit(solution)/shard_map/ppermute | solution.py:384
  48.1 22.5 %collective-permute-start.3 = (f32[264,768]{1,0:T(8,128)S(1)}, f32[264,768]{1,0:T(8,128)S(1)}, u32[]{:S(2)}, u32[]{:S(2)}) collective-permute-start(f32[264,768]{1,0:T(8,128)S(1)} %add_add_fusion.1.a_ref), channel_id=1, source_target_pairs={{0,96},{1,97},{2,98},{3,99},{4,100},{5,101},{6,102},{7,103},{8,104... | collective-permute-start | bytes 2433032 | tf_op jit(solution)/shard_map/ppermute | solution.py:384
  56.2 14.4 %collective-permute-start.7 = (f32[128,768]{1,0:T(8,128)S(1)}, f32[128,768]{1,0:T(8,128)S(1)}, u32[]{:S(2)}, u32[]{:S(2)}) collective-permute-start(f32[128,768]{1,0:T(8,128)S(1)} %add_add_fusion.2.ca_ref), channel_id=1, source_target_pairs={{0,96},{1,97},{2,98},{3,99},{8,104},{9,105},{10,106},{11,107},{16,... | collective-permute-start | bytes 1179656 | tf_op jit(solution)/shard_map/ppermute | solution.py:384
  57.6 13.0 %copy-start = (f32[3,1,512]{2,1,0:T(1,128)S(1)}, f32[3,1,512]{2,1,0:T(1,128)}, u32[]{:S(2)}) copy-start(f32[3,1,512]{2,1,0:T(1,128)} %ridge_ref.3) | copy-start | bytes 18436
where the time goes:
time: 90.6 us; the launch traced here: 90 us
  Pallas kernels  35.7 us (39%)
  waiting for transfers between devices  32.3 us (36%)
  starting transfers between devices  14.6 us (16%)
  other arithmetic  5.45 us (6%)
  between operations  1.06 us (1%)
  local copies, waits for them, and re-layouts  0.93 us (1%)
    ppermute x12, waiting for transfers between devices, moved(): return lax.ppermute(block, ('row', 'col'), links)  32.3 us
    pallas_call x1, Pallas kernels, second_step(): pl.pallas_call(second_kernel, out_shape=(shaped(count, NB), shaped(count,...  19.2 us
    ppermute x12, starting transfers between devices, moved(): return lax.ppermute(block, ('row', 'col'), links)  14.6 us
    pallas_call x1, Pallas kernels, first_step(): pl.pallas_call(first_kernel, out_shape=(shaped(count, 2 * half), shaped(c...  13 us
    pallas_call x1, Pallas kernels, prepare(): pl.pallas_call(prepare_kernel, out_shape=(shaped(half + 8, feat), shaped(...  3.47 us
    add x1, other arithmetic, per_device(): a1 = jnp.where(row_idx == 0, own1, F32(0.0)) + f1 + g1 + h1  1.88 us
  transfers between devices with their start and end apart: 12, of which 3 were waited for; matrix products, arithmetic and copies ran while one was open for 5% of the time, Pallas kernels for 14%

commit v1 on v0

--- a/solution.py
+++ b/solution.py
@@ -121,8 +121,8 @@
 
 def first_kernel(
     where_ref, rows_hbm, a_ref, b_ref,
-    panel_hbm, p_hi, p_lo, pan_hi, pan_lo, line_ref, inv_hi, inv_lo, low_hi, low_lo,
-    rows, kp, out, cols_ref, in_sem, out_sem,
+    panel_hbm, p_hi, p_lo, pan_hi_hbm, pan_lo_hbm, line_ref, inv_hi, inv_lo, low_hi, low_lo,
+    rows, kp, out, pan_hi, pan_lo, cols_ref, in_sem, out_sems,
 ):
     count, feat = rows.shape
     half = kp.shape[1]
@@ -132,6 +132,14 @@
     pan_hi[...], pan_lo[...] = split(a_ref[:half, :] + b_ref[:half, :])
     line = a_ref[half : half + 1, :half] + b_ref[half : half + 1, :half]
     line_ref[...] = jnp.broadcast_to(line, (8, half))
+    stores = [
+        pltpu.make_async_copy(pan_hi, pan_hi_hbm, out_sems.at[0]),
+        pltpu.make_async_copy(pan_lo, pan_lo_hbm, out_sems.at[1]),
+        pltpu.make_async_copy(out.at[0], panel_hbm.at[:, pl.ds(0, NB)], out_sems.at[2]),
+        pltpu.make_async_copy(out.at[1], panel_hbm.at[:, pl.ds(NB, NB)], out_sems.at[3]),
+    ]
+    stores[0].start()
+    stores[1].start()
     pan = (pan_hi[...], pan_lo[...])
     k11 = kernel_tile(pan, (pan_hi[:NB, :], pan_lo[:NB, :]), 0, line[:, :NB], feat)
     k22 = kernel_tile(
@@ -157,36 +165,43 @@
     def solve(i):
         n = i * STEP
         x = dot3(split(kp[n : n + STEP, :NB]), (inv_hi[0], inv_lo[0]))
-        out[n : n + STEP, :NB] = x
+        out[0, n : n + STEP, :] = x
         hi, lo = split(x)
         p_hi[n : n + STEP, :NB], p_lo[n : n + STEP, :NB] = hi, lo
         kp[n : n + STEP, NB:] = kp[n : n + STEP, NB:] - dot3((hi, lo), (low_hi[...], low_lo[...]))
 
     _, inv = factor(s11, cols_ref, [lambda i=i: solve(i) for i in range(count // STEP)])
+    stores[2].start()
     inv_hi[1], inv_lo[1] = split(jnp.concatenate(inv, axis=0))
     x = dot3(split(kp[:, NB:]), (inv_hi[1], inv_lo[1]))
-    out[:, NB:] = x
+    out[1] = x
+    stores[3].start()
     p_hi[:, NB:], p_lo[:, NB:] = split(x)
-    store = pltpu.make_async_copy(out, panel_hbm.at[:, pl.ds(0, half)], out_sem)
-    store.start()
-    store.wait()
+    for store in stores:
+        store.wait()
 
 
 def second_kernel(
-    where_ref, rows_hbm, a_ref, b_ref, ca_ref, cb_ref, ridge_ref, old_panel,
-    p_hi, p_lo, pan_hi, pan_lo, line_ref, inv_hi, inv_lo, low_hi, low_lo,
+    where_ref, rows_hbm, a_ref, b_ref, ridge_ref, old_panel,
+    p_hi, p_lo, pan_hi_hbm, pan_lo_hbm, line_ref, inv_hi, inv_lo, low_hi, low_lo,
     schur_ref, panel_hbm,
     rows, kp, out, q_hi, q_lo, l2_hi, l2_lo, l32_hi, l32_lo, nv_hi, nv_lo, col_hi, col_lo, kc, pc_hi, pc_lo,
-    cols_ref, in_sem, out_sem,
+    pan_hi, pan_lo, cols_ref, in_sems, out_sems,
 ):
     count, feat = rows.shape
     half = kp.shape[1]
-    load = pltpu.make_async_copy(rows_hbm, rows, in_sem)
-    load.start()
+    early = [
+        pltpu.make_async_copy(pan_hi_hbm, pan_hi, in_sems.at[0]),
+        pltpu.make_async_copy(pan_lo_hbm, pan_lo, in_sems.at[1]),
+    ]
+    load = pltpu.make_async_copy(rows_hbm, rows, in_sems.at[2])
+    for copy in early + [load]:
+        copy.start()
     row_idx, col_idx = where_ref[0], where_ref[1]
     q_hi[...], q_lo[...] = split(a_ref[:half, :] + b_ref[:half, :])
     line = a_ref[half : half + 1, :half] + b_ref[half : half + 1, :half]
-    col_hi[...], col_lo[...] = split(ca_ref[...] + cb_ref[...])
+    tail = half + 8
+    col_hi[...], col_lo[...] = split(a_ref[tail:, :] + b_ref[tail:, :])
     new = (q_hi[...], q_lo[...])
 
     def lead(k, dst_hi, dst_lo):
@@ -197,8 +212,11 @@
         dst_hi[:, :NB], dst_lo[:, :NB] = s0
         dst_hi[:, NB:half], dst_lo[:, NB:half] = s1
 
+    k2 = kernel_tile(new, new, 0, line, feat)
+    for copy in early:
+        copy.wait()
     lead(tile_of(dot3(new, (pan_hi[...], pan_lo[...])), feat), l2_hi, l2_lo)
-    k2 = kernel_tile(new, new, 0, line, feat) - dot3((l2_hi[...], l2_lo[...]), (l2_hi[...], l2_lo[...]))
+    k2 = k2 - dot3((l2_hi[...], l2_lo[...]), (l2_hi[...], l2_lo[...]))
     load.wait()
 
     def tiles(i):
@@ -239,7 +257,7 @@
     def solve(i):
         n = i * STEP
         x = dot3(split(kp[n : n + STEP, :NB]), (nv_hi[0], nv_lo[0]))
-        out[n : n + STEP, :NB] = x
+        out[0, n : n + STEP, :] = x
         s = split(x)
         kp[n : n + STEP, NB:] = kp[n : n + STEP, NB:] - dot3(s, (l32_hi[...], l32_lo[...]))
         g = tile_of(dot3(split(rows[n : n + STEP, :]), (col_hi[...], col_lo[...])), feat)
@@ -254,14 +272,21 @@
     _, inv = factor(
         s33, cols_ref, [columns] + [lambda i=i: solve(i) for i in range(count // STEP)]
     )
+    stores = [
+        pltpu.make_async_copy(
+            out.at[i], panel_hbm.at[:, pl.ds(half + i * NB, NB)], out_sems.at[i]
+        )
+        for i in range(2)
+    ]
+    stores[0].start()
     nv_hi[1], nv_lo[1] = split(jnp.concatenate(inv, axis=0))
     pc = split(dot3(split(kc[:, NB:]), (nv_hi[1], nv_lo[1])))
     x = dot3(split(kp[:, NB:]), (nv_hi[1], nv_lo[1]))
-    out[:, NB:] = x
-    store = pltpu.make_async_copy(out, panel_hbm.at[:, pl.ds(half, half)], out_sem)
-    store.start()
+    out[1] = x
+    stores[1].start()
     schur_ref[...] = schur_ref[...] - dot3(split(x), pc)
-    store.wait()
+    for store in stores:
+        store.wait()
 
 
 VM = pl.BlockSpec(memory_space=pltpu.VMEM)
@@ -291,14 +316,16 @@
             shaped(NB, NB, kind=BF16),
         ),
         in_specs=[SM, HB, VM, VM],
-        out_specs=(HB,) + (VM,) * 9,
+        out_specs=(HB, VM, VM, HB, HB) + (VM,) * 5,
         scratch_shapes=[
             pltpu.VMEM((count, feat), F32),
             pltpu.VMEM((count, half), F32),
-            pltpu.VMEM((count, half), F32),
+            pltpu.VMEM((2, count, NB), F32),
+            pltpu.VMEM((half, feat), BF16),
+            pltpu.VMEM((half, feat), BF16),
             pltpu.VMEM((NB, NB), F32),
             pltpu.SemaphoreType.DMA,
-            pltpu.SemaphoreType.DMA,
+            pltpu.SemaphoreType.DMA((4,)),
         ],
         compiler_params=pltpu.CompilerParams(vmem_limit_bytes=20 << 20),
         cost_estimate=pl.CostEstimate(flops=5 * 10**9, bytes_accessed=40 * 10**6, transcendentals=0),
@@ -306,19 +333,19 @@
     )(where, rows, *pair)
 
 
-def second_step(where, rows, pair, cols, ridge, kept):
+def second_step(where, rows, pair, ridge, kept):
     count, feat = rows.shape
     half = 256
     return pl.pallas_call(
         second_kernel,
         out_shape=(shaped(count, NB), shaped(count, 2 * half)),
-        in_specs=[SM, HB] + [VM] * 5 + [HB] + [VM] * 9,
+        in_specs=[SM, HB] + [VM] * 3 + [HB, VM, VM, HB, HB] + [VM] * 5,
         out_specs=(VM, HB),
-        input_output_aliases={7: 1},
+        input_output_aliases={5: 1},
         scratch_shapes=[
             pltpu.VMEM((count, feat), F32),
             pltpu.VMEM((count, half), F32),
-            pltpu.VMEM((count, half), F32),
+            pltpu.VMEM((2, count, NB), F32),
             pltpu.VMEM((half, feat), BF16),
             pltpu.VMEM((half, feat), BF16),
             pltpu.VMEM((half, half), BF16),
@@ -332,34 +359,49 @@
             pltpu.VMEM((NB, half), F32),
             pltpu.VMEM((NB, half + NB), BF16),
             pltpu.VMEM((NB, half + NB), BF16),
+            pltpu.VMEM((half, feat), BF16),
+            pltpu.VMEM((half, feat), BF16),
             pltpu.VMEM((NB, NB), F32),
-            pltpu.SemaphoreType.DMA,
-            pltpu.SemaphoreType.DMA,
+            pltpu.SemaphoreType.DMA((3,)),
+            pltpu.SemaphoreType.DMA((2,)),
         ],
         compiler_params=pltpu.CompilerParams(vmem_limit_bytes=20 << 20),
         cost_estimate=pl.CostEstimate(flops=5 * 10**9, bytes_accessed=40 * 10**6, transcendentals=0),
         name="second_step",
-    )(where, rows, *pair, *cols, ridge, *kept)
-
-
-def prepare_kernel(where_ref, feats_ref, ridge_ref, own0, own1, piece, sems):
+    )(where, rows, *pair, ridge, *kept)
+
+
+def prepare_kernel(where_ref, feats_ref, ridge_ref, own0, own1, piece, buf, sems):
     half = own0.shape[0] - 8
+    full = half + 8
+    starts = (0, full, 2 * full)
     loads = [
-        pltpu.make_async_copy(feats_ref.at[0, pl.ds(0, half)], own0.at[pl.ds(0, half)], sems.at[0]),
-        pltpu.make_async_copy(feats_ref.at[0, pl.ds(half, half)], own1.at[pl.ds(0, half)], sems.at[1]),
+        pltpu.make_async_copy(feats_ref.at[0, pl.ds(0, half)], buf.at[pl.ds(0, half)], sems.at[0]),
         pltpu.make_async_copy(
-            feats_ref.at[where_ref[1] // 32, pl.ds(pl.multiple_of(where_ref[1] % 4 * NB, NB), NB)],
-            piece,
+            feats_ref.at[0, pl.ds(half, half)], buf.at[pl.ds(full, half)], sems.at[1]
+        ),
+        pltpu.make_async_copy(
+            feats_ref.at[where_ref[2] // 32, pl.ds(pl.multiple_of(where_ref[2] % 4 * NB, NB), NB)],
+            buf.at[pl.ds(2 * full, NB)],
             sems.at[2],
         ),
     ]
+    stores = [
+        pltpu.make_async_copy(buf.at[pl.ds(s, ref.shape[0])], ref, sems.at[3 + i])
+        for i, (s, ref) in enumerate(zip(starts, (own0, own1, piece)))
+    ]
     for load in loads:
         load.start()
-    for h, own in enumerate((own0, own1)):
-        own[half:, :half] = jnp.broadcast_to(ridge_ref[0, :, h * half : (h + 1) * half], (8, half))
-        own[half:, half:] = jnp.zeros((8, own.shape[1] - half), F32)
-    for load in loads:
+    for h in range(2):
+        low = starts[h] + half
+        line = ridge_ref[0, :, h * half : (h + 1) * half]
+        buf[low : low + 8, :half] = jnp.broadcast_to(line, (8, half))
+        buf[low : low + 8, half:] = jnp.zeros((8, buf.shape[1] - half), F32)
+    for load, store in zip(loads, stores):
         load.wait()
+        store.start()
+    for store in stores:
+        store.wait()
 
 
 def prepare(where, feats, ridge):
@@ -368,10 +410,60 @@
         prepare_kernel,
         out_shape=(shaped(half + 8, feat), shaped(half + 8, feat), shaped(NB, feat)),
         in_specs=[SM, HB, VM],
-        out_specs=(VM, VM, VM),
-        scratch_shapes=[pltpu.SemaphoreType.DMA((3,))],
+        out_specs=(ANY, ANY, ANY),
+        scratch_shapes=[
+            pltpu.VMEM((2 * half + 16 + NB, feat), F32),
+            pltpu.SemaphoreType.DMA((6,)),
+        ],
         name="prepare",
     )(where, feats, ridge)
+
+
+def join_kernel(where_ref, own1, f1, g1, h1, piece, got, out, sems):
+    full = own1.shape[0]
+    row_idx, col_idx = where_ref[0], where_ref[1]
+    top, low = out.at[pl.ds(0, full)], out.at[pl.ds(full, piece.shape[0])]
+    mine = row_idx % 2 == col_idx % 8 // 4
+    holder = row_idx == col_idx // 4 % 8
+    picks = [
+        (row_idx == 0, own1, top, 0),
+        (row_idx == 2, f1, top, 0),
+        (row_idx == 6, g1, top, 0),
+        (row_idx == 4, h1, top, 0),
+        (holder, piece, low, 1),
+        (mine & jnp.logical_not(holder), got, low, 1),
+    ]
+    for test, src, dst, i in picks:
+
+        @pl.when(test)
+        def _(src=src, dst=dst, i=i):
+            pltpu.make_async_copy(src, dst, sems.at[i]).start()
+
+    @pl.when(row_idx % 2 == 1)
+    def _():
+        top[...] = jnp.zeros(top.shape, F32)
+
+    @pl.when(jnp.logical_not(mine))
+    def _():
+        low[...] = jnp.zeros(low.shape, F32)
+
+    for test, src, dst, i in picks:
+
+        @pl.when(test)
+        def _(src=src, dst=dst, i=i):
+            pltpu.make_async_copy(src, dst, sems.at[i]).wait()
+
+
+def join(where, *parts):
+    rows = parts[0].shape[0] + parts[4].shape[0]
+    return pl.pallas_call(
+        join_kernel,
+        out_shape=shaped(rows, parts[0].shape[1]),
+        in_specs=[SM] + [ANY] * 6,
+        out_specs=VM,
+        scratch_shapes=[pltpu.SemaphoreType.DMA((2,))],
+        name="join",
+    )(where, *parts)
 
 
 def moved(block, hop):
@@ -380,44 +472,50 @@
         x, c, z, y = device // 192, device // 96 % 2, device % 96 // 8, device % 8
         to = hop(x, c, y, z)
         if to is not None:
-            links.append((device, (to[0] % 4 * 2 + to[1]) * 96 + z * 8 + y))
+            near = (z + (to[2] if len(to) > 2 else 0)) % 12
+            links.append((device, (to[0] % 4 * 2 + to[1]) * 96 + near * 8 + y))
     return lax.ppermute(block, ("row", "col"), links)
+
+
+ANY = pl.BlockSpec(memory_space=pl.ANY)
 
 
 def along(start, stop):
     return lambda x, c, y, z: (stop, 0) if (x, c) == (start, 0) else None
 
 
-def fanned(step):
-    return lambda x, c, y, z: (x + step, c) if (x, c) == (z % 4, y // 4) else None
+def fanned(x, c, y, z):
+    turn = (x - z) % 4
+    if turn == 2 or c != y // 4:
+        return None
+    return {0: (x + 1, c, 0), 3: (x - 1, c, -1), 1: (x + 2, c, 1)}[turn]
 
 
 def per_device(features, ridge):
     tiles, _, width, feat = features.shape
     row_idx = lax.axis_index("row")
     col_idx = lax.axis_index("col")
-    where = jnp.stack([row_idx, col_idx]).astype(jnp.int32)
+    turn = (row_idx // 2 - col_idx // 8) % 4
+    near = (col_idx // 8 + jnp.where(turn == 1, 1, jnp.where(turn == 3, -1, 0))) % 12
+    where = jnp.stack([row_idx, col_idx, near * 8 + col_idx % 8]).astype(jnp.int32)
     feats = features.reshape(tiles, width, feat)
     own0, own1, piece = prepare(where, feats, ridge)
     g0 = moved(own0, along(0, 3))
     f0 = moved(own0, along(0, 1))
     d0 = moved(own0, along(0, 2))
-    g1 = moved(own1, along(0, 3))
     f1 = moved(own1, along(0, 1))
-    c1 = moved(piece, fanned(1))
-    c2 = moved(piece, fanned(3))
-    c3 = moved(piece, fanned(2))
     a0 = jnp.where(row_idx == 0, own0, F32(0.0)) + f0 + g0 + d0
     b0 = moved(a0, lambda x, c, y, z: (x, 1) if c == 0 else None)
-    h1 = moved(g1, along(3, 2))
-    rows = pltpu.with_memory_space_constraint(feats.reshape(tiles * width, feat), pltpu.HBM)
+    g1 = moved(own1, along(0, 3))
+    got = moved(piece, fanned)
+    h1 = moved(f1, along(1, 2))
+    rows = pltpu.with_memory_space_constraint(
+        feats.reshape(tiles * width, feat), pltpu.HBM
+    )
     kept = first_step(where, rows, (a0, b0))
-    a1 = jnp.where(row_idx == 0, own1, F32(0.0)) + f1 + g1 + h1
-    b1 = moved(a1, lambda x, c, y, z: (x, 1) if c == 0 else None)
-    holder = row_idx == col_idx // 4 % 8
-    ca = jnp.where(holder, piece, F32(0.0)) + c1 + c2 + c3
-    cb = moved(ca, lambda x, c, y, z: (x, 1 - c) if c == y // 4 else None)
-    schur, panel = second_step(where, rows, (a1, b1), (ca, cb), ridge, kept)
+    a1 = join(where, own1, f1, g1, h1, piece, got)
+    b1 = moved(a1, lambda x, c, y, z: (x, 1 - c))
+    schur, panel = second_step(where, rows, (a1, b1), ridge, kept)
     return (
         schur.reshape(tiles, 1, width, 1, 1, NB),
         panel.reshape(tiles, 1, width, width),

time: 90.6 us -> 88 us (0.971)
  the two profiles are of different devices: /device:TPU:2 before, /device:TPU:1 now
where the time goes in v1:
time: 88 us; the launch traced here: 87.4 us
  starting transfers between devices  50.4 us (57%)
  Pallas kernels  35 us (40%)
  between operations  1.03 us (1%)
  other arithmetic  0.91 us (1%)
    ppermute x9, starting transfers between devices, moved(): return lax.ppermute(block, ('row', 'col'), links)  50.4 us
    pallas_call x1, Pallas kernels, second_step(): pl.pallas_call(second_kernel, out_shape=(shaped(count, NB), shaped(count,...  18.1 us
    pallas_call x1, Pallas kernels, first_step(): pl.pallas_call(first_kernel, out_shape=(shaped(count, 2 * half), shaped(c...  11.9 us
    pallas_call x1, Pallas kernels, prepare(): pl.pallas_call(prepare_kernel, out_shape=(shaped(half + 8, feat), shaped(...  3.16 us
    pallas_call x1, Pallas kernels, join(): pl.pallas_call(join_kernel, out_shape=shaped(rows, parts[0].shape[1]), in...  1.83 us
  transfers between devices with their start and end apart: 9, of which 0 were waited for; matrix products, arithmetic and copies ran while one was open for 0% of the time, Pallas kernels for 16%

profile of v1, /device:TPU:1, one launch (start us, length us, event | category | flops | bytes accessed | tf_op | source)
XLA Modules:
  0.0 87.4 jit_solution(5712574872637240589)
XLA Ops:
  0.7 0.7 pad_add_fusion.where_ref
  1.4 3.2 %prepare.1 = (f32[264,768]{1,0:T(8,128)}, f32[264,768]{1,0:T(8,128)}, f32[128,768]{1,0:T(8,128)}) custom-call(s32[3]{0:T(128)} %pad_add_fusion.where_ref, f32[3,512,768]{2,1,0:T(8,128)} %bitcast.11, f32[3,1,512]{2,1,0:T(1,128)} %ridge_ref.3), custom_call_target="tpu_custom_call" | custom-call | tf_op jit(solution)/shard_map/prepare/pallas_call | solution.py:409
  4.5 1.6 %collective-permute-start = (f32[264,768]{1,0:T(8,128)}, f32[264,768]{1,0:T(8,128)}, u32[]{:S(2)}, u32[]{:S(2)}) collective-permute-start(f32[264,768]{1,0:T(8,128)} %get-tuple-element.17.own1), channel_id=1, source_target_pairs={{0,192},{1,193},{2,194},{3,195},{4,196},{5,197},{6,198},{7,199},{8... | collective-permute-start | bytes 2433032 | tf_op jit(solution)/shard_map/ppermute | solution.py:477
  6.1 0.7 collective-permute-start.7
  6.8 0.7 collective-permute-start.6
  7.5 0.7 collective-permute-start.5
  8.3 1.6 %collective-permute-start.1 = (f32[264,768]{1,0:T(8,128)}, f32[264,768]{1,0:T(8,128)}, u32[]{:S(2)}, u32[]{:S(2)}) collective-permute-start(f32[264,768]{1,0:T(8,128)} %get-tuple-element.17.own1), channel_id=1, source_target_pairs={{0,576},{1,577},{2,578},{3,579},{4,580},{5,581},{6,582},{7,583},{8... | collective-permute-start | bytes 2433032 | tf_op jit(solution)/shard_map/ppermute | solution.py:477
  9.8 0.0 collective-permute-done.f1
  9.8 1.6 %collective-permute-start.2 = (f32[264,768]{1,0:T(8,128)}, f32[264,768]{1,0:T(8,128)}, u32[]{:S(2)}, u32[]{:S(2)}) collective-permute-start(f32[264,768]{1,0:T(8,128)} %collective-permute-done.f1), channel_id=1, source_target_pairs={{192,384},{193,385},{194,386},{195,387},{196,388},{197,389},{198,3... | collective-permute-start | bytes 2433032 | tf_op jit(solution)/shard_map/ppermute | solution.py:477
  11.4 0.0 collective-permute-done.7
  11.4 1.4 %collective-permute-start.3 = (f32[128,768]{1,0:T(8,128)}, f32[128,768]{1,0:T(8,128)}, u32[]{:S(2)}, u32[]{:S(2)}) collective-permute-start(f32[128,768]{1,0:T(8,128)} %get-tuple-element.18.piece), channel_id=1, source_target_pairs={{0,192},{1,193},{2,194},{3,195},{8,576},{9,577},{10,578},{11,579},... | collective-permute-start | bytes 1179656 | tf_op jit(solution)/shard_map/ppermute | solution.py:477
  12.8 0.0 collective-permute-done.6
  12.8 0.0 collective-permute-done.5
  12.8 0.3 add_add_fusion.a_ref
  13.1 0.0 copy-start.2
  13.1 1.3 %collective-permute-start.8 = (f32[264,768]{1,0:T(8,128)S(1)}, f32[264,768]{1,0:T(8,128)S(1)}, u32[]{:S(2)}, u32[]{:S(2)}) collective-permute-start(f32[264,768]{1,0:T(8,128)S(1)} %add_add_fusion.a_ref), channel_id=1, source_target_pairs={{0,96},{1,97},{2,98},{3,99},{4,100},{5,101},{6,102},{7,103},{8,104... | collective-permute-start | bytes 2433032 | tf_op jit(solution)/shard_map/ppermute | solution.py:477
  14.4 0.0 collective-permute-done.3.got
  14.4 0.0 collective-permute-done.1.g1
  14.4 0.0 collective-permute-done.2.h1
  14.4 1.8 %join.1.a_ref = f32[392,768]{1,0:T(8,128)} custom-call(s32[3]{0:T(128)} %pad_add_fusion.where_ref, f32[264,768]{1,0:T(8,128)} %get-tuple-element.17.own1, f32[264,768]{1,0:T(8,128)} %collective-permute-done.f1, f32[264,768]{1,0:T(8,128)} %collective-permute-done.1.g1, f32[264,768]{1,0:T(8,128)} %collective-permute-done.2.h1, ...), custom_call_target="tpu_custom_call" | custom-call | tf_op jit(solution)/shard_map/join/pallas_call | solution.py:459
  16.2 40.9 %collective-permute-start.4 = (f32[392,768]{1,0:T(8,128)}, f32[392,768]{1,0:T(8,128)S(1)}, u32[]{:S(2)}, u32[]{:S(2)}) collective-permute-start(f32[392,768]{1,0:T(8,128)} %join.1.a_ref), channel_id=1, source_target_pairs={{0,96},{1,97},{2,98},{3,99},{4,100},{5,101},{6,102},{7,103},{8,104... | collective-permute-start | bytes 3612680 | tf_op jit(solution)/shard_map/ppermute | solution.py:477
  57.1 0.0 collective-permute-done.8.b_ref
  57.1 0.0 copy-done.2
  57.1 0.0 copy-start
  57.2 0.0 copy-start.1
  57.2 11.9 %first_step.1 = (f32[1536,512]{1,0:T(8,128)}, bf16[1536,256]{1,0:T(8,128)(2,1)S(1)}, bf16[1536,256]{1,0:T(8,128)(2,1)S(1)}, bf16[256,768]{1,0:T(8,128)(2,1)S(1)}...) custom-call(s32[3]{0:T(128)S(1)} %copy-done.2, ...), custom_call_target="tpu_custom_call" | custom-call | flops 5000000000 | bytes 40000000 | tf_op jit(solution)/shard_map/first_step/pallas_call | solution.py:304
  69.1 0.0 collective-permute-done.4.b_ref
  69.1 0.0 copy-done
  69.1 0.0 copy-done.1
  69.1 18.1 %second_step.1 = (f32[1536,128]{1,0:T(8,128)}, f32[1536,512]{1,0:T(8,128)}) custom-call(s32[3]{0:T(128)S(1)} %copy-done.2, f32[1536,768]{1,0:T(8,128)} %bitcast.13, f32[392,768]{1,0:T(8,128)S(1)} %copy-done, f32[392,768]{1,0:T(8,128)S(1)} %collective-permute-done.4.b_ref, f32[3,1,512]{2,1,0:T(1,128)S(1)} %copy-done.1, ...), custom_call_target="tpu_custom_call", output_to_operand_aliasing={{1}: (5, {})} | custom-call | flops 5000000000 | bytes 40000000 | tf_op jit(solution)/shard_map/second_step/pallas_call | solution.py:339
Async XLA Ops:
  4.5 5.3 %collective-permute-start = (f32[264,768]{1,0:T(8,128)}, f32[264,768]{1,0:T(8,128)}, u32[]{:S(2)}, u32[]{:S(2)}) collective-permute-start(f32[264,768]{1,0:T(8,128)} %get-tuple-element.17.own1), channel_id=1, source_target_pairs={{0,192},{1,193},{2,194},{3,195},{4,196},{5,197},{6,198},{7,199},{8... | collective-permute-start | bytes 2433032 | tf_op jit(solution)/shard_map/ppermute | solution.py:477
  6.1 5.3 %collective-permute-start.7 = (f32[264,768]{1,0:T(8,128)}, f32[264,768]{1,0:T(8,128)S(1)}, u32[]{:S(2)}, u32[]{:S(2)}) collective-permute-start(f32[264,768]{1,0:T(8,128)} %get-tuple-element.19), channel_id=1, source_target_pairs={{0,384},{1,385},{2,386},{3,387},{4,388},{5,389},{6,390},{7,391},{8... | collective-permute-start | bytes 2433032 | tf_op jit(solution)/shard_map/ppermute | solution.py:477
  6.8 6.0 %collective-permute-start.6 = (f32[264,768]{1,0:T(8,128)}, f32[264,768]{1,0:T(8,128)S(1)}, u32[]{:S(2)}, u32[]{:S(2)}) collective-permute-start(f32[264,768]{1,0:T(8,128)} %get-tuple-element.19), channel_id=1, source_target_pairs={{0,576},{1,577},{2,578},{3,579},{4,580},{5,581},{6,582},{7,583},{8... | collective-permute-start | bytes 2433032 | tf_op jit(solution)/shard_map/ppermute | solution.py:477
  7.5 5.3 %collective-permute-start.5 = (f32[264,768]{1,0:T(8,128)}, f32[264,768]{1,0:T(8,128)S(1)}, u32[]{:S(2)}, u32[]{:S(2)}) collective-permute-start(f32[264,768]{1,0:T(8,128)} %get-tuple-element.19), channel_id=1, source_target_pairs={{0,192},{1,193},{2,194},{3,195},{4,196},{5,197},{6,198},{7,199},{8... | collective-permute-start | bytes 2433032 | tf_op jit(solution)/shard_map/ppermute | solution.py:477
  8.3 6.1 %collective-permute-start.1 = (f32[264,768]{1,0:T(8,128)}, f32[264,768]{1,0:T(8,128)}, u32[]{:S(2)}, u32[]{:S(2)}) collective-permute-start(f32[264,768]{1,0:T(8,128)} %get-tuple-element.17.own1), channel_id=1, source_target_pairs={{0,576},{1,577},{2,578},{3,579},{4,580},{5,581},{6,582},{7,583},{8... | collective-permute-start | bytes 2433032 | tf_op jit(solution)/shard_map/ppermute | solution.py:477
  9.8 4.6 %collective-permute-start.2 = (f32[264,768]{1,0:T(8,128)}, f32[264,768]{1,0:T(8,128)}, u32[]{:S(2)}, u32[]{:S(2)}) collective-permute-start(f32[264,768]{1,0:T(8,128)} %collective-permute-done.f1), channel_id=1, source_target_pairs={{192,384},{193,385},{194,386},{195,387},{196,388},{197,389},{198,3... | collective-permute-start | bytes 2433032 | tf_op jit(solution)/shard_map/ppermute | solution.py:477
  11.4 3.0 %collective-permute-start.3 = (f32[128,768]{1,0:T(8,128)}, f32[128,768]{1,0:T(8,128)}, u32[]{:S(2)}, u32[]{:S(2)}) collective-permute-start(f32[128,768]{1,0:T(8,128)} %get-tuple-element.18.piece), channel_id=1, source_target_pairs={{0,192},{1,193},{2,194},{3,195},{8,576},{9,577},{10,578},{11,579},... | collective-permute-start | bytes 1179656 | tf_op jit(solution)/shard_map/ppermute | solution.py:477
  13.1 44.1 %copy-start.2 = (s32[3]{0:T(128)S(1)}, s32[3]{0:T(128)}, u32[]{:S(2)}) copy-start(s32[3]{0:T(128)} %pad_add_fusion.where_ref) | copy-start | bytes 40
  13.1 44.0 %collective-permute-start.8 = (f32[264,768]{1,0:T(8,128)S(1)}, f32[264,768]{1,0:T(8,128)S(1)}, u32[]{:S(2)}, u32[]{:S(2)}) collective-permute-start(f32[264,768]{1,0:T(8,128)S(1)} %add_add_fusion.a_ref), channel_id=1, source_target_pairs={{0,96},{1,97},{2,98},{3,99},{4,100},{5,101},{6,102},{7,103},{8,104... | collective-permute-start | bytes 2433032 | tf_op jit(solution)/shard_map/ppermute | solution.py:477
  16.2 52.8 %collective-permute-start.4 = (f32[392,768]{1,0:T(8,128)}, f32[392,768]{1,0:T(8,128)S(1)}, u32[]{:S(2)}, u32[]{:S(2)}) collective-permute-start(f32[392,768]{1,0:T(8,128)} %join.1.a_ref), channel_id=1, source_target_pairs={{0,96},{1,97},{2,98},{3,99},{4,100},{5,101},{6,102},{7,103},{8,104... | collective-permute-start | bytes 3612680 | tf_op jit(solution)/shard_map/ppermute | solution.py:477
  57.1 11.9 %copy-start = (f32[392,768]{1,0:T(8,128)S(1)}, f32[392,768]{1,0:T(8,128)}, u32[]{:S(2)}) copy-start(f32[392,768]{1,0:T(8,128)} %join.1.a_ref) | copy-start | bytes 3612676
  57.2 11.9 %copy-start.1 = (f32[3,1,512]{2,1,0:T(1,128)S(1)}, f32[3,1,512]{2,1,0:T(1,128)}, u32[]{:S(2)}) copy-start(f32[3,1,512]{2,1,0:T(1,128)} %ridge_ref.3) | copy-start | bytes 18436

commit v2 on v1

--- a/solution.py
+++ b/solution.py
@@ -120,7 +120,7 @@
 
 
 def first_kernel(
-    where_ref, rows_hbm, a_ref, b_ref,
+    where_ref, rows_hbm, aa_ref, ab_ref, ba_ref, bb_ref,
     panel_hbm, p_hi, p_lo, pan_hi_hbm, pan_lo_hbm, line_ref, inv_hi, inv_lo, low_hi, low_lo,
     rows, kp, out, pan_hi, pan_lo, cols_ref, in_sem, out_sems,
 ):
@@ -129,8 +129,9 @@
     load = pltpu.make_async_copy(rows_hbm, rows, in_sem)
     load.start()
     row_idx = where_ref[0]
-    pan_hi[...], pan_lo[...] = split(a_ref[:half, :] + b_ref[:half, :])
-    line = a_ref[half : half + 1, :half] + b_ref[half : half + 1, :half]
+    pan_hi[:NB, :], pan_lo[:NB, :] = split(aa_ref[...] + ba_ref[...])
+    pan_hi[NB:, :], pan_lo[NB:, :] = split(ab_ref[:NB, :] + bb_ref[:NB, :])
+    line = ab_ref[NB : NB + 1, :half] + bb_ref[NB : NB + 1, :half]
     line_ref[...] = jnp.broadcast_to(line, (8, half))
     stores = [
         pltpu.make_async_copy(pan_hi, pan_hi_hbm, out_sems.at[0]),
@@ -182,7 +183,7 @@
 
 
 def second_kernel(
-    where_ref, rows_hbm, a_ref, b_ref, ridge_ref, old_panel,
+    where_ref, rows_hbm, a_ref, b_ref, h_ref, piece_ref, got_ref, ridge_ref, old_panel,
     p_hi, p_lo, pan_hi_hbm, pan_lo_hbm, line_ref, inv_hi, inv_lo, low_hi, low_lo,
     schur_ref, panel_hbm,
     rows, kp, out, q_hi, q_lo, l2_hi, l2_lo, l32_hi, l32_lo, nv_hi, nv_lo, col_hi, col_lo, kc, pc_hi, pc_lo,
@@ -198,10 +199,11 @@
     for copy in early + [load]:
         copy.start()
     row_idx, col_idx = where_ref[0], where_ref[1]
-    q_hi[...], q_lo[...] = split(a_ref[:half, :] + b_ref[:half, :])
-    line = a_ref[half : half + 1, :half] + b_ref[half : half + 1, :half]
-    tail = half + 8
-    col_hi[...], col_lo[...] = split(a_ref[tail:, :] + b_ref[tail:, :])
+    q_hi[...], q_lo[...] = split(a_ref[:half, :] + b_ref[:half, :] + h_ref[:half, :])
+    end = half + 1
+    line = a_ref[half:end, :half] + b_ref[half:end, :half] + h_ref[half:end, :half]
+    holder = row_idx == col_idx // 4 % 8
+    col_hi[...], col_lo[...] = split(jnp.where(holder, piece_ref[...], got_ref[...]))
     new = (q_hi[...], q_lo[...])
 
     def lead(k, dst_hi, dst_lo):
@@ -298,7 +300,7 @@
     return jax.ShapeDtypeStruct(shape, kind)
 
 
-def first_step(where, rows, pair):
+def first_step(where, rows, parts):
     count, feat = rows.shape
     half = 256
     return pl.pallas_call(
@@ -315,7 +317,7 @@
             shaped(NB, NB, kind=BF16),
             shaped(NB, NB, kind=BF16),
         ),
-        in_specs=[SM, HB, VM, VM],
+        in_specs=[SM, HB] + [VM] * 4,
         out_specs=(HB, VM, VM, HB, HB) + (VM,) * 5,
         scratch_shapes=[
             pltpu.VMEM((count, feat), F32),
@@ -330,18 +332,18 @@
         compiler_params=pltpu.CompilerParams(vmem_limit_bytes=20 << 20),
         cost_estimate=pl.CostEstimate(flops=5 * 10**9, bytes_accessed=40 * 10**6, transcendentals=0),
         name="first_step",
-    )(where, rows, *pair)
-
-
-def second_step(where, rows, pair, ridge, kept):
+    )(where, rows, *parts)
+
+
+def second_step(where, rows, parts, ridge, kept):
     count, feat = rows.shape
     half = 256
     return pl.pallas_call(
         second_kernel,
         out_shape=(shaped(count, NB), shaped(count, 2 * half)),
-        in_specs=[SM, HB] + [VM] * 3 + [HB, VM, VM, HB, HB] + [VM] * 5,
+        in_specs=[SM, HB] + [VM] * 6 + [HB, VM, VM, HB, HB] + [VM] * 5,
         out_specs=(VM, HB),
-        input_output_aliases={5: 1},
+        input_output_aliases={8: 1},
         scratch_shapes=[
             pltpu.VMEM((count, feat), F32),
             pltpu.VMEM((count, half), F32),
@@ -368,15 +370,16 @@
         compiler_params=pltpu.CompilerParams(vmem_limit_bytes=20 << 20),
         cost_estimate=pl.CostEstimate(flops=5 * 10**9, bytes_accessed=40 * 10**6, transcendentals=0),
         name="second_step",
-    )(where, rows, *pair, ridge, *kept)
-
-
-def prepare_kernel(where_ref, feats_ref, ridge_ref, own0, own1, piece, buf, sems):
-    half = own0.shape[0] - 8
+    )(where, rows, *parts, ridge, *kept)
+
+
+def prepare_kernel(where_ref, feats_ref, ridge_ref, own0a, own0b, own1, piece, buf, sems):
+    half = own1.shape[0] - 8
     full = half + 8
     starts = (0, full, 2 * full)
     loads = [
-        pltpu.make_async_copy(feats_ref.at[0, pl.ds(0, half)], buf.at[pl.ds(0, half)], sems.at[0]),
+        pltpu.make_async_copy(feats_ref.at[0, pl.ds(0, NB)], buf.at[pl.ds(0, NB)], sems.at[0]),
+        pltpu.make_async_copy(feats_ref.at[0, pl.ds(NB, NB)], buf.at[pl.ds(NB, NB)], sems.at[3]),
         pltpu.make_async_copy(
             feats_ref.at[0, pl.ds(half, half)], buf.at[pl.ds(full, half)], sems.at[1]
         ),
@@ -387,8 +390,8 @@
         ),
     ]
     stores = [
-        pltpu.make_async_copy(buf.at[pl.ds(s, ref.shape[0])], ref, sems.at[3 + i])
-        for i, (s, ref) in enumerate(zip(starts, (own0, own1, piece)))
+        pltpu.make_async_copy(buf.at[pl.ds(s, ref.shape[0])], ref, sems.at[4 + i])
+        for i, (s, ref) in enumerate(zip((0, NB) + starts[1:], (own0a, own0b, own1, piece)))
     ]
     for load in loads:
         load.start()
@@ -408,62 +411,15 @@
     half, feat = 256, feats.shape[2]
     return pl.pallas_call(
         prepare_kernel,
-        out_shape=(shaped(half + 8, feat), shaped(half + 8, feat), shaped(NB, feat)),
+        out_shape=(shaped(NB, feat), shaped(NB + 8, feat), shaped(half + 8, feat), shaped(NB, feat)),
         in_specs=[SM, HB, VM],
-        out_specs=(ANY, ANY, ANY),
+        out_specs=(ANY, ANY, ANY, ANY),
         scratch_shapes=[
             pltpu.VMEM((2 * half + 16 + NB, feat), F32),
-            pltpu.SemaphoreType.DMA((6,)),
+            pltpu.SemaphoreType.DMA((8,)),
         ],
         name="prepare",
     )(where, feats, ridge)
-
-
-def join_kernel(where_ref, own1, f1, g1, h1, piece, got, out, sems):
-    full = own1.shape[0]
-    row_idx, col_idx = where_ref[0], where_ref[1]
-    top, low = out.at[pl.ds(0, full)], out.at[pl.ds(full, piece.shape[0])]
-    mine = row_idx % 2 == col_idx % 8 // 4
-    holder = row_idx == col_idx // 4 % 8
-    picks = [
-        (row_idx == 0, own1, top, 0),
-        (row_idx == 2, f1, top, 0),
-        (row_idx == 6, g1, top, 0),
-        (row_idx == 4, h1, top, 0),
-        (holder, piece, low, 1),
-        (mine & jnp.logical_not(holder), got, low, 1),
-    ]
-    for test, src, dst, i in picks:
-
-        @pl.when(test)
-        def _(src=src, dst=dst, i=i):
-            pltpu.make_async_copy(src, dst, sems.at[i]).start()
-
-    @pl.when(row_idx % 2 == 1)
-    def _():
-        top[...] = jnp.zeros(top.shape, F32)
-
-    @pl.when(jnp.logical_not(mine))
-    def _():
-        low[...] = jnp.zeros(low.shape, F32)
-
-    for test, src, dst, i in picks:
-
-        @pl.when(test)
-        def _(src=src, dst=dst, i=i):
-            pltpu.make_async_copy(src, dst, sems.at[i]).wait()
-
-
-def join(where, *parts):
-    rows = parts[0].shape[0] + parts[4].shape[0]
-    return pl.pallas_call(
-        join_kernel,
-        out_shape=shaped(rows, parts[0].shape[1]),
-        in_specs=[SM] + [ANY] * 6,
-        out_specs=VM,
-        scratch_shapes=[pltpu.SemaphoreType.DMA((2,))],
-        name="join",
-    )(where, *parts)
 
 
 def moved(block, hop):
@@ -473,7 +429,8 @@
         to = hop(x, c, y, z)
         if to is not None:
             near = (z + (to[2] if len(to) > 2 else 0)) % 12
-            links.append((device, (to[0] % 4 * 2 + to[1]) * 96 + near * 8 + y))
+            flat = to[3] if len(to) > 3 else y
+            links.append((device, (to[0] % 4 * 2 + to[1]) * 96 + near * 8 + flat))
     return lax.ppermute(block, ("row", "col"), links)
 
 
@@ -486,36 +443,48 @@
 
 def fanned(x, c, y, z):
     turn = (x - z) % 4
-    if turn == 2 or c != y // 4:
+    same = y // 4 == c
+    if turn == 2 and same:
         return None
-    return {0: (x + 1, c, 0), 3: (x - 1, c, -1), 1: (x + 2, c, 1)}[turn]
+    step, lift = {0: (1, 0), 3: (-1, -1), 1: (2, 1), 2: (0, 2)}[turn]
+    return (x + step, c if same else 1 - c, lift, y if same else 7 - y)
 
 
 def per_device(features, ridge):
     tiles, _, width, feat = features.shape
     row_idx = lax.axis_index("row")
     col_idx = lax.axis_index("col")
-    turn = (row_idx // 2 - col_idx // 8) % 4
-    near = (col_idx // 8 + jnp.where(turn == 1, 1, jnp.where(turn == 3, -1, 0))) % 12
-    where = jnp.stack([row_idx, col_idx, near * 8 + col_idx % 8]).astype(jnp.int32)
+    y, z = col_idx % 8, col_idx // 8
+    turn = (row_idx // 2 - z) % 4
+    lift = jnp.where(turn == 1, 1, jnp.where(turn == 3, -1, jnp.where(turn == 2, 2, 0)))
+    flat = jnp.where(y // 4 == row_idx % 2, y, 7 - y)
+    where = jnp.stack([row_idx, col_idx, (z + lift) % 12 * 8 + flat]).astype(jnp.int32)
     feats = features.reshape(tiles, width, feat)
-    own0, own1, piece = prepare(where, feats, ridge)
-    g0 = moved(own0, along(0, 3))
-    f0 = moved(own0, along(0, 1))
-    d0 = moved(own0, along(0, 2))
+    own0a, own0b, own1, piece = prepare(where, feats, ridge)
+    lead = row_idx == 0
+    zero = F32(0.0)
+    down = lambda x, c, y, z: (x, 1) if c == 0 else None
+    f0a = moved(own0a, along(0, 1))
+    g0b = moved(own0b, along(0, 3))
+    f0b = moved(own0b, along(0, 1))
+    g0a = moved(own0a, along(0, 3))
     f1 = moved(own1, along(0, 1))
-    a0 = jnp.where(row_idx == 0, own0, F32(0.0)) + f0 + g0 + d0
-    b0 = moved(a0, lambda x, c, y, z: (x, 1) if c == 0 else None)
     g1 = moved(own1, along(0, 3))
+    ha = moved(f0a, along(1, 2))
+    hb = moved(g0b, along(3, 2))
+    a0a = jnp.where(lead, own0a, zero) + f0a + g0a + ha
+    a0b = jnp.where(lead, own0b, zero) + f0b + g0b + hb
+    b0a = moved(a0a, down)
+    b0b = moved(a0b, down)
+    a1 = jnp.where(lead, own1, zero) + f1 + g1
+    b1 = moved(a1, lambda x, c, y, z: (x, 1) if c == 0 and x != 2 else None)
+    h1 = moved(a1, lambda x, c, y, z: (2, x // 2) if c == 0 and x % 2 else None)
     got = moved(piece, fanned)
-    h1 = moved(f1, along(1, 2))
     rows = pltpu.with_memory_space_constraint(
         feats.reshape(tiles * width, feat), pltpu.HBM
     )
-    kept = first_step(where, rows, (a0, b0))
-    a1 = join(where, own1, f1, g1, h1, piece, got)
-    b1 = moved(a1, lambda x, c, y, z: (x, 1 - c))
-    schur, panel = second_step(where, rows, (a1, b1), ridge, kept)
+    kept = first_step(where, rows, (a0a, a0b, b0a, b0b))
+    schur, panel = second_step(where, rows, (a1, b1, h1, piece, got), ridge, kept)
     return (
         schur.reshape(tiles, 1, width, 1, 1, NB),
         panel.reshape(tiles, 1, width, width),

time: 88 us -> 102 us (1.16)
  the two profiles are of different devices: /device:TPU:1 before, /device:TPU:3 now
where the time goes in v2:
time: 102 us; the launch traced here: 101 us
  starting transfers between devices  39 us (38%)
  Pallas kernels  33.3 us (33%)
  waiting for transfers between devices  24.3 us (24%)
  other arithmetic  3.35 us (3%)
  between operations  1.13 us (1%)
    ppermute x13, starting transfers between devices, moved(): return lax.ppermute(block, ('row', 'col'), links)  39 us
    ppermute x13, waiting for transfers between devices, moved(): return lax.ppermute(block, ('row', 'col'), links)  24.3 us
    pallas_call x1, Pallas kernels, second_step(): pl.pallas_call(second_kernel, out_shape=(shaped(count, NB), shaped(count,...  18.2 us
    pallas_call x1, Pallas kernels, first_step(): pl.pallas_call(first_kernel, out_shape=(shaped(count, 2 * half), shaped(c...  11.9 us
    pallas_call x1, Pallas kernels, prepare(): pl.pallas_call(prepare_kernel, out_shape=(shaped(NB, feat), shaped(NB + 8...  3.16 us
  transfers between devices with their start and end apart: 13, of which 2 were waited for; matrix products, arithmetic and copies ran while one was open for 3% of the time, Pallas kernels for 12%

profile of v2, /device:TPU:3, one launch (start us, length us, event | category | flops | bytes accessed | tf_op | source)
XLA Modules:
  0.0 101.1 jit_solution(5770792560184386324)
XLA Ops:
  0.7 0.7 pad_add_fusion.where_ref
  1.4 3.2 %prepare.1 = (f32[128,768]{1,0:T(8,128)}, f32[136,768]{1,0:T(8,128)}, f32[264,768]{1,0:T(8,128)}, f32[128,768]{1,0:T(8,128)}) custom-call(s32[3]{0:T(128)} %pad_add_fusion.where_ref, f32[3,512,768]{2,1,0:T(8,128)} %bitcast.11, f32[3,1,512]{2,1,0:T(1,128)} %ridge_ref.3), custom_call_target="tpu_custom_call" | custom-call | tf_op jit(solution)/shard_map/prepare/pallas_call | solution.py:412
  4.6 0.0 copy-start.3
  4.6 1.5 %collective-permute-start.5 = (f32[128,768]{1,0:T(8,128)}, f32[128,768]{1,0:T(8,128)}, u32[]{:S(2)}, u32[]{:S(2)}) collective-permute-start(f32[128,768]{1,0:T(8,128)} %get-tuple-element.20), channel_id=1, source_target_pairs={{0,192},{1,193},{2,194},{3,195},{4,196},{5,197},{6,198},{7,199},{8... | collective-permute-start | bytes 1179656 | tf_op jit(solution)/shard_map/ppermute | solution.py:434
  6.1 0.7 collective-permute-start.9
  6.8 0.7 collective-permute-start.6
  7.5 0.0 collective-permute-done.5
  7.5 1.4 %collective-permute-start.7 = (f32[128,768]{1,0:T(8,128)}, f32[128,768]{1,0:T(8,128)}, u32[]{:S(2)}, u32[]{:S(2)}) collective-permute-start(f32[128,768]{1,0:T(8,128)} %collective-permute-done.5), channel_id=1, source_target_pairs={{192,384},{193,385},{194,386},{195,387},{196,388},{197,389},{198,3... | collective-permute-start | bytes 1179656 | tf_op jit(solution)/shard_map/ppermute | solution.py:434
  9.0 0.7 collective-permute-start.1
  9.7 0.7 collective-permute-start
  10.4 0.0 collective-permute-done.6
  10.4 0.7 collective-permute-start.8
  11.1 0.0 collective-permute-done.9
  11.1 0.0 copy-done.4
  11.1 1.4 %collective-permute-start.10 = (f32[136,768]{1,0:T(8,128)S(1)}, f32[136,768]{1,0:T(8,128)}, u32[]{:S(2)}, u32[]{:S(2)}) collective-permute-start(f32[136,768]{1,0:T(8,128)S(1)} %collective-permute-done.9), channel_id=1, source_target_pairs={{576,384},{577,385},{578,386},{579,387},{580,388},{581,389},{582,3... | collective-permute-start | bytes 1253384 | tf_op jit(solution)/shard_map/ppermute | solution.py:434
  12.6 0.0 collective-permute-done.7
  12.6 1.3 %add_add_fusion.2.aa_ref = f32[128,768]{1,0:T(8,128)S(1)} fusion(f32[128,768]{1,0:T(8,128)} %collective-permute-done.7, f32[128,768]{1,0:T(8,128)} %copy-done.4, f32[128,768]{1,0:T(8,128)} %collective-permute-done.5, f32[128,768]{1,0:T(8,128)} %get-tuple-element.20, pred[]{:T(512)S(6)} %eq.24), kind=kLoop, calls=%fused_computation.2 | loop fusion | flops 393216 | bytes 1966081 | tf_op jit(solution)/shard_map/add | solution.py:475
  13.9 1.4 %collective-permute-start.11 = (f32[128,768]{1,0:T(8,128)S(1)}, f32[128,768]{1,0:T(8,128)S(1)}, u32[]{:S(2)}, u32[]{:S(2)}) collective-permute-start(f32[128,768]{1,0:T(8,128)S(1)} %add_add_fusion.2.aa_ref), channel_id=1, source_target_pairs={{0,96},{1,97},{2,98},{3,99},{4,100},{5,101},{6,102},{7,103},{8,104... | collective-permute-start | bytes 1179656 | tf_op jit(solution)/shard_map/ppermute | solution.py:434
  15.3 0.0 collective-permute-done.8
  15.4 1.2 %add_add_fusion.1.ab_ref = f32[136,768]{1,0:T(8,128)S(1)} fusion(f32[136,768]{1,0:T(8,128)} %collective-permute-done.10, f32[136,768]{1,0:T(8,128)S(1)} %collective-permute-done.9, f32[136,768]{1,0:T(8,128)S(1)} %collective-permute-done.8, f32[136,768]{1,0:T(8,128)} %get-tuple-element.21, pred[]{:T(512)S(6)} %eq.24), kind=kLoop, calls=%fused_computation.1 | loop fusion | flops 417792 | bytes 2088961 | tf_op jit(solution)/shard_map/add | solution.py:476
  16.5 1.3 %collective-permute-start.12 = (f32[136,768]{1,0:T(8,128)S(1)}, f32[136,768]{1,0:T(8,128)S(1)}, u32[]{:S(2)}, u32[]{:S(2)}) collective-permute-start(f32[136,768]{1,0:T(8,128)S(1)} %add_add_fusion.1.ab_ref), channel_id=1, source_target_pairs={{0,96},{1,97},{2,98},{3,99},{4,100},{5,101},{6,102},{7,103},{8,104... | collective-permute-start | bytes 1253384 | tf_op jit(solution)/shard_map/ppermute | solution.py:434
  17.8 0.0 collective-permute-done
  17.8 0.2 add_add_fusion.a_ref
  18.0 0.7 collective-permute-start.3
  18.8 1.3 %collective-permute-start.2 = (f32[264,768]{1,0:T(8,128)S(1)}, f32[264,768]{1,0:T(8,128)S(1)}, u32[]{:S(2)}, u32[]{:S(2)}) collective-permute-start(f32[264,768]{1,0:T(8,128)S(1)} %add_add_fusion.a_ref), channel_id=1, source_target_pairs={{0,96},{1,97},{2,98},{3,99},{4,100},{5,101},{6,102},{7,103},{8,104... | collective-permute-start | bytes 2433032 | tf_op jit(solution)/shard_map/ppermute | solution.py:434
  20.1 26.5 %collective-permute-start.4 = (f32[128,768]{1,0:T(8,128)S(1)}, f32[128,768]{1,0:T(8,128)S(1)}, u32[]{:S(2)}, u32[]{:S(2)}) collective-permute-start(f32[128,768]{1,0:T(8,128)S(1)} %copy-done.2), channel_id=1, source_target_pairs={{0,192},{1,193},{2,194},{3,195},{4,291},{5,290},{6,289},{7,288},{8... | collective-permute-start | bytes 1179656 | tf_op jit(solution)/shard_map/ppermute | solution.py:434
  46.6 1.0 collective-permute-done.12.bb_ref
  47.5 11.9 %first_step.1 = (f32[1536,512]{1,0:T(8,128)}, bf16[1536,256]{1,0:T(8,128)(2,1)S(1)}, bf16[1536,256]{1,0:T(8,128)(2,1)S(1)}, bf16[256,768]{1,0:T(8,128)(2,1)S(1)}...) custom-call(s32[3]{0:T(128)S(1)} %copy-done.1, ...), custom_call_target="tpu_custom_call" | custom-call | flops 5000000000 | bytes 40000000 | tf_op jit(solution)/shard_map/first_step/pallas_call | solution.py:306
  59.4 23.3 %collective-permute-done.4.got_ref = f32[128,768]{1,0:T(8,128)S(1)} collective-permute-done((f32[128,768]{1,0:T(8,128)S(1)}, f32[128,768]{1,0:T(8,128)S(1)}, u32[]{:S(2)}, u32[]{:S(2)}) %collective-permute-start.4) | collective-permute-done | bytes 393248 | tf_op jit(solution)/shard_map/ppermute | solution.py:434
  82.7 0.0 collective-permute-done.3.h_ref
  82.7 0.0 collective-permute-done.2.b_ref
  82.7 18.2 %second_step.1 = (f32[1536,128]{1,0:T(8,128)}, f32[1536,512]{1,0:T(8,128)}) custom-call(s32[3]{0:T(128)S(1)} %copy-done.1, f32[1536,768]{1,0:T(8,128)} %bitcast.13, f32[264,768]{1,0:T(8,128)S(1)} %add_add_fusion.a_ref, f32[264,768]{1,0:T(8,128)S(1)} %collective-permute-done.2.b_ref, ...), custom_call_target="tpu_custom_call", output_to_operand_aliasing={{1}: (8, {})} | custom-call | flops 5000000000 | bytes 40000000 | tf_op jit(solution)/shard_map/second_step/pallas_call | solution.py:341
  (11 shorter events, 0.0 us)
Async XLA Ops:
  4.6 13.2 %copy-start.3 = (f32[264,768]{1,0:T(8,128)S(1)}, f32[264,768]{1,0:T(8,128)}, u32[]{:S(2)}) copy-start(f32[264,768]{1,0:T(8,128)} %get-tuple-element.18) | copy-start | bytes 2433028
  4.6 2.9 %collective-permute-start.5 = (f32[128,768]{1,0:T(8,128)}, f32[128,768]{1,0:T(8,128)}, u32[]{:S(2)}, u32[]{:S(2)}) collective-permute-start(f32[128,768]{1,0:T(8,128)} %get-tuple-element.20), channel_id=1, source_target_pairs={{0,192},{1,193},{2,194},{3,195},{4,196},{5,197},{6,198},{7,199},{8... | collective-permute-start | bytes 1179656 | tf_op jit(solution)/shard_map/ppermute | solution.py:434
  6.1 5.0 %collective-permute-start.9 = (f32[136,768]{1,0:T(8,128)}, f32[136,768]{1,0:T(8,128)S(1)}, u32[]{:S(2)}, u32[]{:S(2)}) collective-permute-start(f32[136,768]{1,0:T(8,128)} %get-tuple-element.21), channel_id=1, source_target_pairs={{0,576},{1,577},{2,578},{3,579},{4,580},{5,581},{6,582},{7,583},{8... | collective-permute-start | bytes 1253384 | tf_op jit(solution)/shard_map/ppermute | solution.py:434
  6.8 3.6 %collective-permute-start.6 = (f32[128,768]{1,0:T(8,128)}, f32[128,768]{1,0:T(8,128)S(1)}, u32[]{:S(2)}, u32[]{:S(2)}) collective-permute-start(f32[128,768]{1,0:T(8,128)} %get-tuple-element.20), channel_id=1, source_target_pairs={{0,576},{1,577},{2,578},{3,579},{4,580},{5,581},{6,582},{7,583},{8... | collective-permute-start | bytes 1179656 | tf_op jit(solution)/shard_map/ppermute | solution.py:434
  7.5 5.0 %collective-permute-start.7 = (f32[128,768]{1,0:T(8,128)}, f32[128,768]{1,0:T(8,128)}, u32[]{:S(2)}, u32[]{:S(2)}) collective-permute-start(f32[128,768]{1,0:T(8,128)} %collective-permute-done.5), channel_id=1, source_target_pairs={{192,384},{193,385},{194,386},{195,387},{196,388},{197,389},{198,3... | collective-permute-start | bytes 1179656 | tf_op jit(solution)/shard_map/ppermute | solution.py:434
  9.0 8.9 %collective-permute-start.1 = (f32[264,768]{1,0:T(8,128)}, f32[264,768]{1,0:T(8,128)S(1)}, u32[]{:S(2)}, u32[]{:S(2)}) collective-permute-start(f32[264,768]{1,0:T(8,128)} %get-tuple-element.18), channel_id=1, source_target_pairs={{0,576},{1,577},{2,578},{3,579},{4,580},{5,581},{6,582},{7,583},{8... | collective-permute-start | bytes 2433032 | tf_op jit(solution)/shard_map/ppermute | solution.py:434
  9.7 8.2 %collective-permute-start = (f32[264,768]{1,0:T(8,128)}, f32[264,768]{1,0:T(8,128)S(1)}, u32[]{:S(2)}, u32[]{:S(2)}) collective-permute-start(f32[264,768]{1,0:T(8,128)} %get-tuple-element.18), channel_id=1, source_target_pairs={{0,192},{1,193},{2,194},{3,195},{4,196},{5,197},{6,198},{7,199},{8... | collective-permute-start | bytes 2433032 | tf_op jit(solution)/shard_map/ppermute | solution.py:434
  10.4 0.7 copy-start.4
  10.4 4.9 %collective-permute-start.8 = (f32[136,768]{1,0:T(8,128)}, f32[136,768]{1,0:T(8,128)S(1)}, u32[]{:S(2)}, u32[]{:S(2)}) collective-permute-start(f32[136,768]{1,0:T(8,128)} %get-tuple-element.21), channel_id=1, source_target_pairs={{0,192},{1,193},{2,194},{3,195},{4,196},{5,197},{6,198},{7,199},{8... | collective-permute-start | bytes 1253384 | tf_op jit(solution)/shard_map/ppermute | solution.py:434
  11.1 4.2 %collective-permute-start.10 = (f32[136,768]{1,0:T(8,128)S(1)}, f32[136,768]{1,0:T(8,128)}, u32[]{:S(2)}, u32[]{:S(2)}) collective-permute-start(f32[136,768]{1,0:T(8,128)S(1)} %collective-permute-done.9), channel_id=1, source_target_pairs={{576,384},{577,385},{578,386},{579,387},{580,388},{581,389},{582,3... | collective-permute-start | bytes 1253384 | tf_op jit(solution)/shard_map/ppermute | solution.py:434
  13.9 6.2 %copy-start.2 = (f32[128,768]{1,0:T(8,128)S(1)}, f32[128,768]{1,0:T(8,128)}, u32[]{:S(2)}) copy-start(f32[128,768]{1,0:T(8,128)} %get-tuple-element.19.piece_ref) | copy-start | bytes 1179652
  13.9 33.6 %copy-start.1 = (s32[3]{0:T(128)S(1)}, s32[3]{0:T(128)}, u32[]{:S(2)}) copy-start(s32[3]{0:T(128)} %pad_add_fusion.where_ref) | copy-start | bytes 40
  13.9 32.7 %collective-permute-start.11 = (f32[128,768]{1,0:T(8,128)S(1)}, f32[128,768]{1,0:T(8,128)S(1)}, u32[]{:S(2)}, u32[]{:S(2)}) collective-permute-start(f32[128,768]{1,0:T(8,128)S(1)} %add_add_fusion.2.aa_ref), channel_id=1, source_target_pairs={{0,96},{1,97},{2,98},{3,99},{4,100},{5,101},{6,102},{7,103},{8,104... | collective-permute-start | bytes 1179656 | tf_op jit(solution)/shard_map/ppermute | solution.py:434
  16.5 31.0 %collective-permute-start.12 = (f32[136,768]{1,0:T(8,128)S(1)}, f32[136,768]{1,0:T(8,128)S(1)}, u32[]{:S(2)}, u32[]{:S(2)}) collective-permute-start(f32[136,768]{1,0:T(8,128)S(1)} %add_add_fusion.1.ab_ref), channel_id=1, source_target_pairs={{0,96},{1,97},{2,98},{3,99},{4,100},{5,101},{6,102},{7,103},{8,104... | collective-permute-start | bytes 1253384 | tf_op jit(solution)/shard_map/ppermute | solution.py:434
  18.0 64.7 %collective-permute-start.3 = (f32[264,768]{1,0:T(8,128)S(1)}, f32[264,768]{1,0:T(8,128)S(1)}, u32[]{:S(2)}, u32[]{:S(2)}) collective-permute-start(f32[264,768]{1,0:T(8,128)S(1)} %add_add_fusion.a_ref), channel_id=1, source_target_pairs={{192,384},{193,385},{194,386},{195,387},{196,388},{197,389},{198,3... | collective-permute-start | bytes 2433032 | tf_op jit(solution)/shard_map/ppermute | solution.py:434
  18.8 64.0 %collective-permute-start.2 = (f32[264,768]{1,0:T(8,128)S(1)}, f32[264,768]{1,0:T(8,128)S(1)}, u32[]{:S(2)}, u32[]{:S(2)}) collective-permute-start(f32[264,768]{1,0:T(8,128)S(1)} %add_add_fusion.a_ref), channel_id=1, source_target_pairs={{0,96},{1,97},{2,98},{3,99},{4,100},{5,101},{6,102},{7,103},{8,104... | collective-permute-start | bytes 2433032 | tf_op jit(solution)/shard_map/ppermute | solution.py:434
  20.1 62.6 %collective-permute-start.4 = (f32[128,768]{1,0:T(8,128)S(1)}, f32[128,768]{1,0:T(8,128)S(1)}, u32[]{:S(2)}, u32[]{:S(2)}) collective-permute-start(f32[128,768]{1,0:T(8,128)S(1)} %copy-done.2), channel_id=1, source_target_pairs={{0,192},{1,193},{2,194},{3,195},{4,291},{5,290},{6,289},{7,288},{8... | collective-permute-start | bytes 1179656 | tf_op jit(solution)/shard_map/ppermute | solution.py:434
  47.5 35.2 %copy-start = (f32[3,1,512]{2,1,0:T(1,128)S(1)}, f32[3,1,512]{2,1,0:T(1,128)}, u32[]{:S(2)}) copy-start(f32[3,1,512]{2,1,0:T(1,128)} %ridge_ref.3) | copy-start | bytes 18436

commit v3 on v2

--- a/solution.py
+++ b/solution.py
@@ -202,8 +202,7 @@
     q_hi[...], q_lo[...] = split(a_ref[:half, :] + b_ref[:half, :] + h_ref[:half, :])
     end = half + 1
     line = a_ref[half:end, :half] + b_ref[half:end, :half] + h_ref[half:end, :half]
-    holder = row_idx == col_idx // 4 % 8
-    col_hi[...], col_lo[...] = split(jnp.where(holder, piece_ref[...], got_ref[...]))
+    col_hi[...], col_lo[...] = split(piece_ref[...] + got_ref[...])
     new = (q_hi[...], q_lo[...])
 
     def lead(k, dst_hi, dst_lo):
@@ -441,24 +440,15 @@
     return lambda x, c, y, z: (stop, 0) if (x, c) == (start, 0) else None
 
 
-def fanned(x, c, y, z):
-    turn = (x - z) % 4
-    same = y // 4 == c
-    if turn == 2 and same:
-        return None
-    step, lift = {0: (1, 0), 3: (-1, -1), 1: (2, 1), 2: (0, 2)}[turn]
-    return (x + step, c if same else 1 - c, lift, y if same else 7 - y)
+def fanned(step):
+    return lambda x, c, y, z: (x + step, c) if (x, c) == (z % 4, y // 4) else None
 
 
 def per_device(features, ridge):
     tiles, _, width, feat = features.shape
     row_idx = lax.axis_index("row")
     col_idx = lax.axis_index("col")
-    y, z = col_idx % 8, col_idx // 8
-    turn = (row_idx // 2 - z) % 4
-    lift = jnp.where(turn == 1, 1, jnp.where(turn == 3, -1, jnp.where(turn == 2, 2, 0)))
-    flat = jnp.where(y // 4 == row_idx % 2, y, 7 - y)
-    where = jnp.stack([row_idx, col_idx, (z + lift) % 12 * 8 + flat]).astype(jnp.int32)
+    where = jnp.stack([row_idx, col_idx, col_idx]).astype(jnp.int32)
     feats = features.reshape(tiles, width, feat)
     own0a, own0b, own1, piece = prepare(where, feats, ridge)
     lead = row_idx == 0
@@ -479,12 +469,17 @@
     a1 = jnp.where(lead, own1, zero) + f1 + g1
     b1 = moved(a1, lambda x, c, y, z: (x, 1) if c == 0 and x != 2 else None)
     h1 = moved(a1, lambda x, c, y, z: (2, x // 2) if c == 0 and x % 2 else None)
-    got = moved(piece, fanned)
+    c1 = moved(piece, fanned(1))
+    c2 = moved(piece, fanned(3))
+    c3 = moved(piece, fanned(2))
     rows = pltpu.with_memory_space_constraint(
         feats.reshape(tiles * width, feat), pltpu.HBM
     )
     kept = first_step(where, rows, (a0a, a0b, b0a, b0b))
-    schur, panel = second_step(where, rows, (a1, b1, h1, piece, got), ridge, kept)
+    holder = row_idx == col_idx // 4 % 8
+    ca = jnp.where(holder, piece, zero) + c1 + c2 + c3
+    cb = moved(ca, lambda x, c, y, z: (x, 1 - c) if c == y // 4 else None)
+    schur, panel = second_step(where, rows, (a1, b1, h1, ca, cb), ridge, kept)
     return (
         schur.reshape(tiles, 1, width, 1, 1, NB),
         panel.reshape(tiles, 1, width, width),

time: 102 us -> 90.6 us (0.89)
  the two profiles are of different devices: /device:TPU:3 before, /device:TPU:2 now
where the time goes in v3:
time: 90.6 us; the launch traced here: 89.9 us
  Pallas kernels  33.8 us (37%)
  waiting for transfers between devices  26.9 us (30%)
  starting transfers between devices  20.3 us (22%)
  other arithmetic  6.01 us (7%)
  local copies, waits for them, and re-layouts  1.68 us (2%)
  between operations  1.16 us (1%)
    ppermute x16, waiting for transfers between devices, moved(): return lax.ppermute(block, ('row', 'col'), links)  26.9 us
    ppermute x16, starting transfers between devices, moved(): return lax.ppermute(block, ('row', 'col'), links)  20.3 us
    pallas_call x1, Pallas kernels, second_step(): pl.pallas_call(second_kernel, out_shape=(shaped(count, NB), shaped(count,...  18.2 us
    pallas_call x1, Pallas kernels, first_step(): pl.pallas_call(first_kernel, out_shape=(shaped(count, 2 * half), shaped(c...  12.5 us
    pallas_call x1, Pallas kernels, prepare(): pl.pallas_call(prepare_kernel, out_shape=(shaped(NB, feat), shaped(NB + 8...  3.16 us
  transfers between devices with their start and end apart: 16, of which 2 were waited for; matrix products, arithmetic and copies ran while one was open for 6% of the time, Pallas kernels for 14%

profile of v3, /device:TPU:2, one launch (start us, length us, event | category | flops | bytes accessed | tf_op | source)
XLA Modules:
  0.0 89.9 jit_solution(5280878104430039438)
XLA Ops:
  0.6 0.7 pad_add_fusion.where_ref
  1.3 3.2 %prepare.1 = (f32[128,768]{1,0:T(8,128)}, f32[136,768]{1,0:T(8,128)}, f32[264,768]{1,0:T(8,128)}, f32[128,768]{1,0:T(8,128)}) custom-call(s32[3]{0:T(128)} %pad_add_fusion.where_ref, f32[3,512,768]{2,1,0:T(8,128)} %bitcast.10, f32[3,1,512]{2,1,0:T(1,128)} %ridge_ref.3), custom_call_target="tpu_custom_call" | custom-call | tf_op jit(solution)/shard_map/prepare/pallas_call | solution.py:411
  4.5 0.0 copy-start.2
  4.5 1.4 %collective-permute-start.8 = (f32[128,768]{1,0:T(8,128)}, f32[128,768]{1,0:T(8,128)S(1)}, u32[]{:S(2)}, u32[]{:S(2)}) collective-permute-start(f32[128,768]{1,0:T(8,128)} %get-tuple-element.20), channel_id=1, source_target_pairs={{0,192},{1,193},{2,194},{3,195},{4,196},{5,197},{6,198},{7,199},{8... | collective-permute-start | bytes 1179656 | tf_op jit(solution)/shard_map/ppermute | solution.py:433
  5.9 0.7 collective-permute-start.12
  6.6 0.7 collective-permute-start.9
  7.3 14.1 %collective-permute-done.8 = f32[128,768]{1,0:T(8,128)S(1)} collective-permute-done((f32[128,768]{1,0:T(8,128)}, f32[128,768]{1,0:T(8,128)S(1)}, u32[]{:S(2)}, u32[]{:S(2)}) %collective-permute-start.8) | collective-permute-done | bytes 393248 | tf_op jit(solution)/shard_map/ppermute | solution.py:433
  21.4 2.0 %collective-permute-start.10 = (f32[128,768]{1,0:T(8,128)S(1)}, f32[128,768]{1,0:T(8,128)}, u32[]{:S(2)}, u32[]{:S(2)}) collective-permute-start(f32[128,768]{1,0:T(8,128)S(1)} %collective-permute-done.8), channel_id=1, source_target_pairs={{192,384},{193,385},{194,386},{195,387},{196,388},{197,389},{198,3... | collective-permute-start | bytes 1179656 | tf_op jit(solution)/shard_map/ppermute | solution.py:433
  23.4 0.7 collective-permute-start.1
  24.1 1.3 %collective-permute-start = (f32[264,768]{1,0:T(8,128)}, f32[264,768]{1,0:T(8,128)S(1)}, u32[]{:S(2)}, u32[]{:S(2)}) collective-permute-start(f32[264,768]{1,0:T(8,128)} %get-tuple-element.18), channel_id=1, source_target_pairs={{0,192},{1,193},{2,194},{3,195},{4,196},{5,197},{6,198},{7,199},{8... | collective-permute-start | bytes 2433032 | tf_op jit(solution)/shard_map/ppermute | solution.py:433
  25.4 1.3 %collective-permute-start.11 = (f32[136,768]{1,0:T(8,128)}, f32[136,768]{1,0:T(8,128)}, u32[]{:S(2)}, u32[]{:S(2)}) collective-permute-start(f32[136,768]{1,0:T(8,128)} %get-tuple-element.21), channel_id=1, source_target_pairs={{0,192},{1,193},{2,194},{3,195},{4,196},{5,197},{6,198},{7,199},{8... | collective-permute-start | bytes 1253384 | tf_op jit(solution)/shard_map/ppermute | solution.py:433
  26.8 1.4 %collective-permute-start.13 = (f32[136,768]{1,0:T(8,128)S(1)}, f32[136,768]{1,0:T(8,128)}, u32[]{:S(2)}, u32[]{:S(2)}) collective-permute-start(f32[136,768]{1,0:T(8,128)S(1)} %collective-permute-done.12), channel_id=1, source_target_pairs={{576,384},{577,385},{578,386},{579,387},{580,388},{581,389},{582,3... | collective-permute-start | bytes 1253384 | tf_op jit(solution)/shard_map/ppermute | solution.py:433
  28.2 0.7 collective-permute-start.6
  28.9 1.3 %add_add_fusion.2.aa_ref = f32[128,768]{1,0:T(8,128)S(1)} fusion(f32[128,768]{1,0:T(8,128)} %collective-permute-done.10, f32[128,768]{1,0:T(8,128)} %copy-done.8, f32[128,768]{1,0:T(8,128)} %copy-done.7, f32[128,768]{1,0:T(8,128)} %get-tuple-element.20, pred[]{:T(512)S(6)} %eq.8), kind=kLoop, calls=%fused_computation.2 | loop fusion | flops 393216 | bytes 1966081 | tf_op jit(solution)/shard_map/add | solution.py:465
  30.2 12.8 %collective-permute-done.11 = f32[136,768]{1,0:T(8,128)} collective-permute-done((f32[136,768]{1,0:T(8,128)}, f32[136,768]{1,0:T(8,128)}, u32[]{:S(2)}, u32[]{:S(2)}) %collective-permute-start.11) | collective-permute-done | bytes 417824 | tf_op jit(solution)/shard_map/ppermute | solution.py:433
  43.1 0.7 collective-permute-start.5
  43.8 1.3 %collective-permute-start.4 = (f32[128,768]{1,0:T(8,128)}, f32[128,768]{1,0:T(8,128)}, u32[]{:S(2)}, u32[]{:S(2)}) collective-permute-start(f32[128,768]{1,0:T(8,128)} %get-tuple-element.19), channel_id=1, source_target_pairs={{0,192},{1,193},{2,194},{3,195},{32,224},{33,225},{34,226},{35,227... | collective-permute-start | bytes 1179656 | tf_op jit(solution)/shard_map/ppermute | solution.py:433
  45.1 1.4 %add_add_fusion.1.ab_ref = f32[136,768]{1,0:T(8,128)S(1)} fusion(f32[136,768]{1,0:T(8,128)} %collective-permute-done.13, f32[136,768]{1,0:T(8,128)} %copy-done.4, f32[136,768]{1,0:T(8,128)} %collective-permute-done.11, f32[136,768]{1,0:T(8,128)} %get-tuple-element.21, pred[]{:T(512)S(6)} %eq.8), kind=kLoop, calls=%fused_computation.1 | loop fusion | flops 417792 | bytes 2088961 | tf_op jit(solution)/shard_map/add | solution.py:466
  46.4 2.1 %collective-permute-start.14 = (f32[128,768]{1,0:T(8,128)S(1)}, f32[128,768]{1,0:T(8,128)}, u32[]{:S(2)}, u32[]{:S(2)}) collective-permute-start(f32[128,768]{1,0:T(8,128)S(1)} %add_add_fusion.2.aa_ref), channel_id=1, source_target_pairs={{0,96},{1,97},{2,98},{3,99},{4,100},{5,101},{6,102},{7,103},{8,104... | collective-permute-start | bytes 1179656 | tf_op jit(solution)/shard_map/ppermute | solution.py:433
  48.5 0.9 %copy-done.3 = f32[264,768]{1,0:T(8,128)} copy-done((f32[264,768]{1,0:T(8,128)}, f32[264,768]{1,0:T(8,128)S(1)}, u32[]{:S(2)}) %copy-start.3) | copy-done | bytes 811032
  49.4 2.0 %collective-permute-start.15 = (f32[136,768]{1,0:T(8,128)S(1)}, f32[136,768]{1,0:T(8,128)}, u32[]{:S(2)}, u32[]{:S(2)}) collective-permute-start(f32[136,768]{1,0:T(8,128)S(1)} %add_add_fusion.1.ab_ref), channel_id=1, source_target_pairs={{0,96},{1,97},{2,98},{3,99},{4,100},{5,101},{6,102},{7,103},{8,104... | collective-permute-start | bytes 1253384 | tf_op jit(solution)/shard_map/ppermute | solution.py:433
  51.4 1.4 %add_add_fusion.a_ref = f32[264,768]{1,0:T(8,128)S(1)} fusion(f32[264,768]{1,0:T(8,128)S(1)} %collective-permute-done.1, f32[264,768]{1,0:T(8,128)} %copy-done.3, f32[264,768]{1,0:T(8,128)S(1)} %copy-done.2, pred[]{:T(512)S(6)} %eq.8), kind=kLoop, calls=%fused_computation | loop fusion | flops 608256 | bytes 3244033 | tf_op jit(solution)/shard_map/add | solution.py:469
  52.8 0.0 copy-start.5
  52.8 1.3 %collective-permute-start.3 = (f32[264,768]{1,0:T(8,128)S(1)}, f32[264,768]{1,0:T(8,128)S(1)}, u32[]{:S(2)}, u32[]{:S(2)}) collective-permute-start(f32[264,768]{1,0:T(8,128)S(1)} %add_add_fusion.a_ref), channel_id=1, source_target_pairs={{192,384},{193,385},{194,386},{195,387},{196,388},{197,389},{198,3... | collective-permute-start | bytes 2433032 | tf_op jit(solution)/shard_map/ppermute | solution.py:433
  54.2 0.0 copy-start.6
  54.2 0.7 copy-done.6
  54.9 1.3 %collective-permute-start.2 = (f32[264,768]{1,0:T(8,128)S(1)}, f32[264,768]{1,0:T(8,128)S(1)}, u32[]{:S(2)}, u32[]{:S(2)}) collective-permute-start(f32[264,768]{1,0:T(8,128)S(1)} %add_add_fusion.a_ref), channel_id=1, source_target_pairs={{0,96},{1,97},{2,98},{3,99},{4,100},{5,101},{6,102},{7,103},{8,104... | collective-permute-start | bytes 2433032 | tf_op jit(solution)/shard_map/ppermute | solution.py:433
  56.3 1.3 %add_add_fusion.3.piece_ref = f32[128,768]{1,0:T(8,128)S(1)} fusion(f32[128,768]{1,0:T(8,128)} %copy-done.5, f32[128,768]{1,0:T(8,128)} %copy-done.6, f32[128,768]{1,0:T(8,128)} %collective-permute-done.4, f32[128,768]{1,0:T(8,128)} %get-tuple-element.19, pred[]{:T(512)S(6)} %eq.9), kind=kLoop, calls=%fused_computation.3 | loop fusion | flops 393216 | bytes 1966081 | tf_op jit(solution)/shard_map/add | solution.py:480
  57.7 1.3 %collective-permute-start.7 = (f32[128,768]{1,0:T(8,128)S(1)}, f32[128,768]{1,0:T(8,128)S(1)}, u32[]{:S(2)}, u32[]{:S(2)}) collective-permute-start(f32[128,768]{1,0:T(8,128)S(1)} %add_add_fusion.3.piece_ref), channel_id=1, source_target_pairs={{0,96},{1,97},{2,98},{3,99},{8,104},{9,105},{10,106},{11,107},{16,... | collective-permute-start | bytes 1179656 | tf_op jit(solution)/shard_map/ppermute | solution.py:433
  59.0 0.0 copy-start
  59.0 12.5 %first_step.1 = (f32[1536,512]{1,0:T(8,128)}, bf16[1536,256]{1,0:T(8,128)(2,1)S(1)}, bf16[1536,256]{1,0:T(8,128)(2,1)S(1)}, bf16[256,768]{1,0:T(8,128)(2,1)S(1)}...) custom-call(s32[3]{0:T(128)S(1)} %copy-done.1, ...), custom_call_target="tpu_custom_call" | custom-call | flops 5000000000 | bytes 40000000 | tf_op jit(solution)/shard_map/first_step/pallas_call | solution.py:305
  71.6 18.2 %second_step.1 = (f32[1536,128]{1,0:T(8,128)}, f32[1536,512]{1,0:T(8,128)}) custom-call(s32[3]{0:T(128)S(1)} %copy-done.1, f32[1536,768]{1,0:T(8,128)} %bitcast.12, f32[264,768]{1,0:T(8,128)S(1)} %add_add_fusion.a_ref, f32[264,768]{1,0:T(8,128)S(1)} %collective-permute-done.2.b_ref, ...), custom_call_target="tpu_custom_call", output_to_operand_aliasing={{1}: (8, {})} | custom-call | flops 5000000000 | bytes 40000000 | tf_op jit(solution)/shard_map/second_step/pallas_call | solution.py:340
  (26 shorter events, 0.1 us)
Async XLA Ops:
  4.5 47.0 %copy-start.2 = (f32[264,768]{1,0:T(8,128)S(1)}, f32[264,768]{1,0:T(8,128)}, u32[]{:S(2)}) copy-start(f32[264,768]{1,0:T(8,128)} %get-tuple-element.18) | copy-start | bytes 2433028
  4.5 16.9 %collective-permute-start.8 = (f32[128,768]{1,0:T(8,128)}, f32[128,768]{1,0:T(8,128)S(1)}, u32[]{:S(2)}, u32[]{:S(2)}) collective-permute-start(f32[128,768]{1,0:T(8,128)} %get-tuple-element.20), channel_id=1, source_target_pairs={{0,192},{1,193},{2,194},{3,195},{4,196},{5,197},{6,198},{7,199},{8... | collective-permute-start | bytes 1179656 | tf_op jit(solution)/shard_map/ppermute | solution.py:433
  5.9 20.8 %collective-permute-start.12 = (f32[136,768]{1,0:T(8,128)}, f32[136,768]{1,0:T(8,128)S(1)}, u32[]{:S(2)}, u32[]{:S(2)}) collective-permute-start(f32[136,768]{1,0:T(8,128)} %get-tuple-element.21), channel_id=1, source_target_pairs={{0,576},{1,577},{2,578},{3,579},{4,580},{5,581},{6,582},{7,583},{8... | collective-permute-start | bytes 1253384 | tf_op jit(solution)/shard_map/ppermute | solution.py:433
  6.6 18.8 %collective-permute-start.9 = (f32[128,768]{1,0:T(8,128)}, f32[128,768]{1,0:T(8,128)S(1)}, u32[]{:S(2)}, u32[]{:S(2)}) collective-permute-start(f32[128,768]{1,0:T(8,128)} %get-tuple-element.20), channel_id=1, source_target_pairs={{0,576},{1,577},{2,578},{3,579},{4,580},{5,581},{6,582},{7,583},{8... | collective-permute-start | bytes 1179656 | tf_op jit(solution)/shard_map/ppermute | solution.py:433
  21.4 6.8 %copy-start.7 = (f32[128,768]{1,0:T(8,128)}, f32[128,768]{1,0:T(8,128)S(1)}, u32[]{:S(2)}) copy-start(f32[128,768]{1,0:T(8,128)S(1)} %collective-permute-done.8) | copy-start | bytes 1179652
  21.4 6.8 %collective-permute-start.10 = (f32[128,768]{1,0:T(8,128)S(1)}, f32[128,768]{1,0:T(8,128)}, u32[]{:S(2)}, u32[]{:S(2)}) collective-permute-start(f32[128,768]{1,0:T(8,128)S(1)} %collective-permute-done.8), channel_id=1, source_target_pairs={{192,384},{193,385},{194,386},{195,387},{196,388},{197,389},{198,3... | collective-permute-start | bytes 1179656 | tf_op jit(solution)/shard_map/ppermute | solution.py:433
  23.4 23.0 %collective-permute-start.1 = (f32[264,768]{1,0:T(8,128)}, f32[264,768]{1,0:T(8,128)S(1)}, u32[]{:S(2)}, u32[]{:S(2)}) collective-permute-start(f32[264,768]{1,0:T(8,128)} %get-tuple-element.18), channel_id=1, source_target_pairs={{0,576},{1,577},{2,578},{3,579},{4,580},{5,581},{6,582},{7,583},{8... | collective-permute-start | bytes 2433032 | tf_op jit(solution)/shard_map/ppermute | solution.py:433
  24.1 24.4 %collective-permute-start = (f32[264,768]{1,0:T(8,128)}, f32[264,768]{1,0:T(8,128)S(1)}, u32[]{:S(2)}, u32[]{:S(2)}) collective-permute-start(f32[264,768]{1,0:T(8,128)} %get-tuple-element.18), channel_id=1, source_target_pairs={{0,192},{1,193},{2,194},{3,195},{4,196},{5,197},{6,198},{7,199},{8... | collective-permute-start | bytes 2433032 | tf_op jit(solution)/shard_map/ppermute | solution.py:433
  25.4 1.3 %copy-start.8 = (f32[128,768]{1,0:T(8,128)}, f32[128,768]{1,0:T(8,128)S(1)}, u32[]{:S(2)}) copy-start(f32[128,768]{1,0:T(8,128)S(1)} %collective-permute-done.9) | copy-start | bytes 1179652
  25.4 17.6 %collective-permute-start.11 = (f32[136,768]{1,0:T(8,128)}, f32[136,768]{1,0:T(8,128)}, u32[]{:S(2)}, u32[]{:S(2)}) collective-permute-start(f32[136,768]{1,0:T(8,128)} %get-tuple-element.21), channel_id=1, source_target_pairs={{0,192},{1,193},{2,194},{3,195},{4,196},{5,197},{6,198},{7,199},{8... | collective-permute-start | bytes 1253384 | tf_op jit(solution)/shard_map/ppermute | solution.py:433
  26.8 17.0 %copy-start.4 = (f32[136,768]{1,0:T(8,128)}, f32[136,768]{1,0:T(8,128)S(1)}, u32[]{:S(2)}) copy-start(f32[136,768]{1,0:T(8,128)S(1)} %collective-permute-done.12) | copy-start | bytes 1253380
  26.8 17.0 %collective-permute-start.13 = (f32[136,768]{1,0:T(8,128)S(1)}, f32[136,768]{1,0:T(8,128)}, u32[]{:S(2)}, u32[]{:S(2)}) collective-permute-start(f32[136,768]{1,0:T(8,128)S(1)} %collective-permute-done.12), channel_id=1, source_target_pairs={{576,384},{577,385},{578,386},{579,387},{580,388},{581,389},{582,3... | collective-permute-start | bytes 1253384 | tf_op jit(solution)/shard_map/ppermute | solution.py:433
  28.2 24.6 %collective-permute-start.6 = (f32[128,768]{1,0:T(8,128)}, f32[128,768]{1,0:T(8,128)S(1)}, u32[]{:S(2)}, u32[]{:S(2)}) collective-permute-start(f32[128,768]{1,0:T(8,128)} %get-tuple-element.19), channel_id=1, source_target_pairs={{0,384},{1,385},{2,386},{3,387},{32,416},{33,417},{34,418},{35,419... | collective-permute-start | bytes 1179656 | tf_op jit(solution)/shard_map/ppermute | solution.py:433
  43.1 11.1 %collective-permute-start.5 = (f32[128,768]{1,0:T(8,128)}, f32[128,768]{1,0:T(8,128)S(1)}, u32[]{:S(2)}, u32[]{:S(2)}) collective-permute-start(f32[128,768]{1,0:T(8,128)} %get-tuple-element.19), channel_id=1, source_target_pairs={{0,576},{1,577},{2,578},{3,579},{32,608},{33,609},{34,610},{35,611... | collective-permute-start | bytes 1179656 | tf_op jit(solution)/shard_map/ppermute | solution.py:433
  43.8 12.6 %collective-permute-start.4 = (f32[128,768]{1,0:T(8,128)}, f32[128,768]{1,0:T(8,128)}, u32[]{:S(2)}, u32[]{:S(2)}) collective-permute-start(f32[128,768]{1,0:T(8,128)} %get-tuple-element.19), channel_id=1, source_target_pairs={{0,192},{1,193},{2,194},{3,195},{32,224},{33,225},{34,226},{35,227... | collective-permute-start | bytes 1179656 | tf_op jit(solution)/shard_map/ppermute | solution.py:433
  46.4 12.6 %copy-start.1 = (s32[3]{0:T(128)S(1)}, s32[3]{0:T(128)}, u32[]{:S(2)}) copy-start(s32[3]{0:T(128)} %pad_add_fusion.where_ref) | copy-start | bytes 40
  46.4 12.5 %collective-permute-start.14 = (f32[128,768]{1,0:T(8,128)S(1)}, f32[128,768]{1,0:T(8,128)}, u32[]{:S(2)}, u32[]{:S(2)}) collective-permute-start(f32[128,768]{1,0:T(8,128)S(1)} %add_add_fusion.2.aa_ref), channel_id=1, source_target_pairs={{0,96},{1,97},{2,98},{3,99},{4,100},{5,101},{6,102},{7,103},{8,104... | collective-permute-start | bytes 1179656 | tf_op jit(solution)/shard_map/ppermute | solution.py:433
  48.5 0.9 %copy-start.3 = (f32[264,768]{1,0:T(8,128)}, f32[264,768]{1,0:T(8,128)S(1)}, u32[]{:S(2)}) copy-start(f32[264,768]{1,0:T(8,128)S(1)} %collective-permute-done) | copy-start | bytes 2433028
  49.4 9.6 %collective-permute-start.15 = (f32[136,768]{1,0:T(8,128)S(1)}, f32[136,768]{1,0:T(8,128)}, u32[]{:S(2)}, u32[]{:S(2)}) collective-permute-start(f32[136,768]{1,0:T(8,128)S(1)} %add_add_fusion.1.ab_ref), channel_id=1, source_target_pairs={{0,96},{1,97},{2,98},{3,99},{4,100},{5,101},{6,102},{7,103},{8,104... | collective-permute-start | bytes 1253384 | tf_op jit(solution)/shard_map/ppermute | solution.py:433
  52.8 1.4 %copy-start.5 = (f32[128,768]{1,0:T(8,128)}, f32[128,768]{1,0:T(8,128)S(1)}, u32[]{:S(2)}) copy-start(f32[128,768]{1,0:T(8,128)S(1)} %collective-permute-done.6) | copy-start | bytes 1179652
  52.8 18.7 %collective-permute-start.3 = (f32[264,768]{1,0:T(8,128)S(1)}, f32[264,768]{1,0:T(8,128)S(1)}, u32[]{:S(2)}, u32[]{:S(2)}) collective-permute-start(f32[264,768]{1,0:T(8,128)S(1)} %add_add_fusion.a_ref), channel_id=1, source_target_pairs={{192,384},{193,385},{194,386},{195,387},{196,388},{197,389},{198,3... | collective-permute-start | bytes 2433032 | tf_op jit(solution)/shard_map/ppermute | solution.py:433
  54.2 0.7 copy-start.6
  54.9 16.6 %collective-permute-start.2 = (f32[264,768]{1,0:T(8,128)S(1)}, f32[264,768]{1,0:T(8,128)S(1)}, u32[]{:S(2)}, u32[]{:S(2)}) collective-permute-start(f32[264,768]{1,0:T(8,128)S(1)} %add_add_fusion.a_ref), channel_id=1, source_target_pairs={{0,96},{1,97},{2,98},{3,99},{4,100},{5,101},{6,102},{7,103},{8,104... | collective-permute-start | bytes 2433032 | tf_op jit(solution)/shard_map/ppermute | solution.py:433
  57.7 13.9 %collective-permute-start.7 = (f32[128,768]{1,0:T(8,128)S(1)}, f32[128,768]{1,0:T(8,128)S(1)}, u32[]{:S(2)}, u32[]{:S(2)}) collective-permute-start(f32[128,768]{1,0:T(8,128)S(1)} %add_add_fusion.3.piece_ref), channel_id=1, source_target_pairs={{0,96},{1,97},{2,98},{3,99},{8,104},{9,105},{10,106},{11,107},{16,... | collective-permute-start | bytes 1179656 | tf_op jit(solution)/shard_map/ppermute | solution.py:433
  59.0 12.5 %copy-start = (f32[3,1,512]{2,1,0:T(1,128)S(1)}, f32[3,1,512]{2,1,0:T(1,128)}, u32[]{:S(2)}) copy-start(f32[3,1,512]{2,1,0:T(1,128)} %ridge_ref.3) | copy-start | bytes 18436
